TPU v7x, 256 devices: a whole 4x4x8 slice. The times are simulated.
256 devices in a mesh: group: 8 (over z), tensor: 32 (over x, y, core).
Axes of the slice: x: 4, y: 4, z: 8, core: 2. Of those that a mesh axis runs over, the one named last changes fastest.
Arguments:
- residual_in: bfloat16 [8192, 2048], P(('group', 'tensor')), parts along dimension 0, may hold values from -22 to 22
- attn_gain: float32 [2048], replicated, may hold values from 0.5 to 1.5
- w_query: bfloat16 [2048, 4096], P(None, 'tensor'), may hold values from -0.125 to 0.125
- w_keyval: bfloat16 [1024, 2048], P('tensor'), may hold values from -0.125 to 0.125
- query_gain: float32 [128], replicated, may hold values from 0.1 to 1.9
- key_gain: float32 [128], replicated, may hold values from 0.1 to 1.9
- w_out: bfloat16 [4096, 2048], P('tensor'), may hold values from -0.09375 to 0.09375
- ffn_gain: float32 [2048], replicated, may hold values from 0.5 to 1.5
- w_gate: bfloat16 [32, 768, 2048], P('tensor'), may hold values from -0.125 to 0.125
- w_up: bfloat16 [32, 768, 2048], P('tensor'), may hold values from -0.125 to 0.125
- w_down: bfloat16 [32, 768, 2048], P('tensor'), may hold values from -0.21875 to 0.21875
- key_cache: bfloat16 [256, 1024, 512], P(('group', 'tensor')), parts along dimension 0, may hold values from -110 to 110
- value_cache: bfloat16 [256, 1024, 512], P(('group', 'tensor')), parts along dimension 0, may hold values from -18 to 18
- prefix_lens: int32 [256], P(('group', 'tensor')), parts along dimension 0, may hold values from 1 to 992
- accepted: int32 [256], P(('group', 'tensor')), parts along dimension 0, may hold values from 1 to 8
- accept_path: int32 [256, 8], P(('group', 'tensor')), parts along dimension 0, may hold values from 0 to 14, as said below
- parents: int32 [256, 32], P(('group', 'tensor')), parts along dimension 0, may hold values from -1 to 30, as said below
- slot_kinds: int32 [256], P(('group', 'tensor')), parts along dimension 0, may hold values from 0 to 1
- expert_ids: int32 [8192, 8], P('group'), parts along dimension 0, may hold values from 0 to 127, as said below
- gate_probs: float32 [8192, 8], P('group'), parts along dimension 0, may hold values from 0.1 to 1
Outputs:
- mixed: bfloat16 [8192, 2048], P(('group', 'tensor')), parts along dimension 0
There are 8 independent parts, one for each index of `group`. A program takes and returns all parts, laid end to end along the dimension named above; an argument that names none is the same for every part. Nothing has to cross between parts.
Inputs may be any that keep to these rules, and one draw needn't show every extreme that they name: `expert_ids`: the tokens of each slot name each of the 128 experts exactly 32 * 8 // 128 times; a token never names one expert twice. `accept_path`: each row starts at 0 and rises by 1 or 2 from one entry to the next. `parents`: node 0 of every slot has parent -1; every other node's parent is an earlier node of the same slot.
All inputs are finite; a program needn't handle non-finite values.
Results may differ from a plain program's by a relative error of at most 0.02.
Values may be sent and summed in bfloat16 or wider, within the bound.
A program may use at most 128 MiB of HBM per device.

v0:
```python
import math

import jax
import jax.numpy as jnp
from jax import lax
from jax.sharding import PartitionSpec as P

EXPERTS = 128
SINK = 4
WIN = 512


EPSILON = 1e-06
NEG_FILL = -1e30
ROPE_BASE = 1000000.0


def rms_rows(values, weight_gain):
    return (
        values
        * lax.rsqrt(jnp.mean(values * values, axis=-1, keepdims=True) + EPSILON)
        * weight_gain
    )


def rotate(values, angles):
    half_dim = values.shape[-1] // 2
    cosine = jnp.cos(angles)[:, None, :]
    sine_val = jnp.sin(angles)[:, None, :]
    lower_half = values[..., :half_dim]
    upper_half = values[..., half_dim:]
    return jnp.concatenate(
        [lower_half * cosine - upper_half * sine_val, upper_half * cosine + lower_half * sine_val],
        axis=-1,
    )


def ancestors(parent_row, count_new):
    parent_link = jax.nn.one_hot(parent_row, count_new, dtype=jnp.float32)
    reach_mat = jnp.eye(count_new, dtype=jnp.float32) + parent_link
    for unused in range((count_new - 1).bit_length()):
        reach_mat = jnp.minimum(jnp.dot(reach_mat, reach_mat, precision=lax.Precision.HIGHEST), 1.0)
    return reach_mat


def attend_parts(
    query_raw,
    keyval_raw,
    key_cache,
    value_cache,
    prefix_len,
    accepted_len,
    path_row,
    parent_row,
    kind_value,
    query_gain,
    key_gain,
):
    count_new = query_raw.shape[0]
    head_dim = query_gain.shape[0]
    kv_heads = key_cache.shape[-1] // head_dim
    q_heads = query_raw.shape[-1] // head_dim
    group_size = q_heads // kv_heads
    cache_len = key_cache.shape[0]
    acc_count = path_row.shape[0]
    total_len = prefix_len + accepted_len
    reach_mat = ancestors(parent_row, count_new)
    index_row = jnp.arange(count_new)
    causal = (index_row[None, :] <= index_row[:, None]).astype(jnp.float32)
    is_tree = kind_value == 1
    allowed = jnp.where(is_tree, reach_mat, causal) > 0.5
    depth_used = jnp.where(is_tree, jnp.sum(reach_mat, axis=1) - 1.0, index_row.astype(jnp.float32))
    position = total_len.astype(jnp.float32) + depth_used
    half_dim = head_dim // 2
    freq_table = jnp.exp(
        -(2.0 * jnp.arange(half_dim, dtype=jnp.float32) / head_dim) * math.log(ROPE_BASE)
    )
    angles = position[:, None] * freq_table[None, :]
    query_rot = rotate(
        rms_rows(query_raw.astype(jnp.float32).reshape(count_new, q_heads, head_dim), query_gain),
        angles,
    ).astype(jnp.bfloat16)
    key_width = kv_heads * head_dim
    key_new = rotate(
        rms_rows(
            keyval_raw[:, :key_width].astype(jnp.float32).reshape(count_new, kv_heads, head_dim),
            key_gain,
        ),
        angles,
    ).astype(jnp.bfloat16)
    value_new = keyval_raw[:, key_width:].reshape(count_new, kv_heads, head_dim)
    acc_rows = prefix_len + path_row
    key_acc = jnp.take(key_cache, acc_rows, axis=0).reshape(acc_count, kv_heads, head_dim)
    value_acc = jnp.take(value_cache, acc_rows, axis=0).reshape(acc_count, kv_heads, head_dim)
    key_old = key_cache.reshape(cache_len, kv_heads, head_dim)
    value_old = value_cache.reshape(cache_len, kv_heads, head_dim)
    cache_pos = jnp.arange(cache_len)
    seen_old = (cache_pos < prefix_len) & ((cache_pos < SINK) | (cache_pos >= total_len - WIN))
    acc_index = jnp.arange(acc_count)
    acc_pos = prefix_len + acc_index
    seen_acc = (acc_index < accepted_len) & ((acc_pos < SINK) | (acc_pos >= total_len - WIN))
    score_scale = head_dim ** (-0.5)
    query_group = query_rot.reshape(count_new, kv_heads, group_size, head_dim)
    score_old = (
        jnp.einsum("nkgd,mkd->kgnm", query_group, key_old, preferred_element_type=jnp.float32)
        * score_scale
    )
    score_acc = (
        jnp.einsum("nkgd,mkd->kgnm", query_group, key_acc, preferred_element_type=jnp.float32)
        * score_scale
    )
    score_new = (
        jnp.einsum("nkgd,mkd->kgnm", query_group, key_new, preferred_element_type=jnp.float32)
        * score_scale
    )
    score_old = jnp.where(seen_old[None, None, None, :], score_old, NEG_FILL)
    score_acc = jnp.where(seen_acc[None, None, None, :], score_acc, NEG_FILL)
    score_new = jnp.where(allowed[None, None], score_new, NEG_FILL)
    row_max = jnp.maximum(
        jnp.maximum(
            jnp.max(score_old, axis=-1, keepdims=True), jnp.max(score_acc, axis=-1, keepdims=True)
        ),
        jnp.max(score_new, axis=-1, keepdims=True),
    )
    expo_old = jnp.exp(score_old - row_max)
    expo_acc = jnp.exp(score_acc - row_max)
    expo_new = jnp.exp(score_new - row_max)
    denom_sum = (
        jnp.sum(expo_old, axis=-1, keepdims=True)
        + jnp.sum(expo_acc, axis=-1, keepdims=True)
        + jnp.sum(expo_new, axis=-1, keepdims=True)
    )
    probs_old = (expo_old / denom_sum).astype(jnp.bfloat16)
    probs_acc = (expo_acc / denom_sum).astype(jnp.bfloat16)
    probs_new = (expo_new / denom_sum).astype(jnp.bfloat16)
    result = jnp.einsum("kgnm,mkd->nkgd", probs_old, value_old, preferred_element_type=jnp.float32)
    result = result + jnp.einsum(
        "kgnm,mkd->nkgd", probs_acc, value_acc, preferred_element_type=jnp.float32
    )
    result = result + jnp.einsum(
        "kgnm,mkd->nkgd", probs_new, value_new, preferred_element_type=jnp.float32
    )
    return result.reshape(count_new, q_heads * head_dim).astype(jnp.bfloat16)


def route_rows(expert_ids, gate_probs, expert_names, count_rows):
    hit_mask = expert_ids[None, :, :] == expert_names[:, None, None]
    weights = jnp.sum(jnp.where(hit_mask, gate_probs[None], 0.0), axis=2)
    named_int = jnp.any(hit_mask, axis=2).astype(jnp.int32)
    chosen = jnp.argsort(1 - named_int, axis=1, stable=True)[:, :count_rows]
    return (chosen, jnp.take_along_axis(weights, chosen, axis=1))


def body(
    residual_in,
    attn_gain,
    w_query,
    w_keyval,
    query_gain,
    key_gain,
    w_out,
    ffn_gain,
    w_gate,
    w_up,
    w_down,
    key_cache,
    value_cache,
    prefix_lens,
    accepted,
    accept_path,
    parents,
    slot_kinds,
    expert_ids,
    gate_probs,
):
    devices = lax.axis_size("tensor")
    own_index = lax.axis_index("tensor")
    rows_here = residual_in.shape[0]
    model_width = residual_in.shape[1]
    slots_here = key_cache.shape[0]
    count_new = rows_here // slots_here
    row_start = own_index * rows_here
    normed_own = rms_rows(residual_in.astype(jnp.float32), attn_gain).astype(jnp.bfloat16)
    gathered = lax.all_gather(normed_own, "tensor", axis=0, tiled=True)
    query_part = jnp.dot(gathered, w_query, preferred_element_type=jnp.float32).astype(jnp.bfloat16)
    keyval_part = lax.dot_general(
        gathered, w_keyval, (((1,), (1,)), ((), ())), preferred_element_type=jnp.float32
    ).astype(jnp.bfloat16)
    query_tok, keyval_tok = (
        lax.all_to_all(query_part, "tensor", split_axis=0, concat_axis=1, tiled=True),
        lax.all_to_all(keyval_part, "tensor", split_axis=0, concat_axis=1, tiled=True),
    )

    def slot_attend(packed):
        return attend_parts(*packed, query_gain, key_gain)

    attn_own = lax.map(
        slot_attend,
        (
            query_tok.reshape(slots_here, count_new, -1),
            keyval_tok.reshape(slots_here, count_new, -1),
            key_cache,
            value_cache,
            prefix_lens,
            accepted,
            accept_path,
            parents,
            slot_kinds,
        ),
    )
    attn_own = attn_own.reshape(rows_here, -1)
    attn_heads = lax.all_to_all(attn_own, "tensor", split_axis=1, concat_axis=0, tiled=True)
    out_own = lax.psum_scatter(
        jnp.dot(attn_heads, w_out, preferred_element_type=jnp.float32).astype(jnp.bfloat16),
        "tensor",
        scatter_dimension=0,
        tiled=True,
    ).astype(jnp.float32)
    hidden_mid = residual_in.astype(jnp.float32) + out_own
    normed_ffn = rms_rows(hidden_mid, ffn_gain).astype(jnp.bfloat16)
    per_device = w_gate.shape[0]
    top_count = expert_ids.shape[1]
    all_names = jnp.arange(per_device * devices, dtype=jnp.int32)
    own_ids = lax.dynamic_slice_in_dim(expert_ids, row_start, rows_here, 0)
    own_gates = lax.dynamic_slice_in_dim(gate_probs, row_start, rows_here, 0)
    chosen, selected = route_rows(own_ids, own_gates, all_names, rows_here * top_count // EXPERTS)
    send_rows = normed_ffn[chosen]
    received = lax.all_to_all(send_rows, "tensor", split_axis=0, concat_axis=0, tiled=True)
    item_count = received.shape[1]
    grouped = received.reshape(devices, per_device, item_count, model_width)
    gate_val = jnp.einsum("spcd,pfd->spcf", grouped, w_gate, preferred_element_type=jnp.float32)
    up_val = jnp.einsum("spcd,pfd->spcf", grouped, w_up, preferred_element_type=jnp.float32)
    inner_act = (jax.nn.silu(gate_val) * up_val).astype(jnp.bfloat16)
    result = jnp.einsum("spcf,pfd->spcd", inner_act, w_down, preferred_element_type=jnp.float32)
    result = result.reshape(devices * per_device, item_count, model_width)
    returned = lax.all_to_all(
        result.astype(jnp.bfloat16), "tensor", split_axis=0, concat_axis=0, tiled=True
    ).astype(result.dtype)
    scaled = returned * selected[..., None]
    moe_own = (
        jnp.zeros((rows_here, model_width), jnp.float32)
        .at[chosen.reshape(-1)]
        .add(scaled.reshape(-1, model_width))
    )
    return (hidden_mid + moe_own).astype(jnp.bfloat16)


def solution(mesh):
    in_specs = (
        P(("group", "tensor"), None),
        P(),
        P(None, "tensor"),
        P("tensor", None),
        P(),
        P(),
        P("tensor", None),
        P(),
        P("tensor", None, None),
        P("tensor", None, None),
        P("tensor", None, None),
        P(("group", "tensor"), None, None),
        P(("group", "tensor"), None, None),
        P(("group", "tensor")),
        P(("group", "tensor")),
        P(("group", "tensor"), None),
        P(("group", "tensor"), None),
        P(("group", "tensor")),
        P("group", None),
        P("group", None),
    )
    out_specs = P(("group", "tensor"), None)
    return jax.shard_map(body, mesh=mesh, in_specs=in_specs, out_specs=out_specs, check_vma=False)
```

profile of v0, /device:TPU:1, one launch (start us, length us, event | category | flops | bytes accessed | tf_op | source)
XLA Modules:
  0.0 284.7 jit_solution(10480858248007846740)
XLA Ops:
  7.7 1.7 fusion.45
  13.8 2.2 reshape.276
  15.9 2.1 reshape.280
  18.7 2.5 gather_fusion.2
  21.2 2.5 gather_fusion.3
  25.1 40.2 %all-gather.2.cloned.1.call-done = bf16[1024,2048]{1,0:T(8,128)(2,1)} async-done(((bf16[32,2048]{1,0:T(8,128)(2,1)}), bf16[1024,2048]{1,0:T(8,128)(2,1)}) %all-gather.2.cloned.1.call-update) | async-done | bytes 4194320 | tf_op jit(solution)/shard_map/all_gather | solution.py:184
  65.3 3.5 %convolution_convert_fusion.2 = bf16[1024,32]{0,1:T(8,128)(2,1)S(1)} fusion(bf16[1024,2048]{1,0:T(8,128)(2,1)} %all-gather.2.cloned.1.call-done, bf16[32,2048]{1,0:T(8,128)(2,1)S(1)} %copy-done.6), kind=kOutput, calls=%fused_computation.38 | convolution fusion | flops 134250496 | bytes 4390912 | tf_op jit(solution)/shard_map/dot_general | solution.py:186
  69.8 5.3 %all-to-all-start.1 = ((bf16[32,2,512]{2,1,0:T(2,128)(2,1)}), bf16[32,2,512]{2,1,0:T(2,128)(2,1)S(1)}, u32[]{:S(2)}, u32[]{:S(2)}) async-start(bf16[32,2,512]{2,1,0:T(2,128)(2,1)} %reshape.354), calls=%async_computation.1 | async-start | bytes 131072 | tf_op jit(solution)/shard_map/all_to_all | solution.py:191
  75.1 4.3 %convolution_convert_fusion.1 = bf16[1024,128]{1,0:T(8,128)(2,1)} fusion(bf16[1024,2048]{1,0:T(8,128)(2,1)} %all-gather.2.cloned.1.call-done, bf16[2048,128]{1,0:T(8,128)(2,1)} %param.24), kind=kOutput, calls=%fused_computation.29 | convolution fusion | flops 537001984 | bytes 4980736 | tf_op jit(solution)/shard_map/dot_general | solution.py:185
  79.4 3.1 %all-to-all-done.1 = bf16[32,2,512]{2,1,0:T(2,128)(2,1)S(1)} async-done(((bf16[32,2,512]{2,1,0:T(2,128)(2,1)}), bf16[32,2,512]{2,1,0:T(2,128)(2,1)S(1)}, u32[]{:S(2)}, u32[]{:S(2)}) %all-to-all-start.1) | async-done | bytes 65568 | tf_op jit(solution)/shard_map/all_to_all | solution.py:191
  82.5 4.3 %all-to-all-start = ((bf16[32,32,128]{2,1,0:T(8,128)(2,1)}), bf16[32,32,128]{2,1,0:T(8,128)(2,1)S(1)}, u32[]{:S(2)}, u32[]{:S(2)}) async-start(bf16[32,32,128]{2,1,0:T(8,128)(2,1)} %bitcast.176), calls=%async_computation | async-start | bytes 524288 | tf_op jit(solution)/shard_map/all_to_all | solution.py:190
  87.7 1.8 copy.200
  94.5 1.4 reshape.282
  98.9 4.0 %bitcast_reduce_fusion = (f32[4,8,32]{1,2,0:T(8,128)S(1)}, f32[4,32,8,1024]{3,2,1,0:T(8,128)}) fusion(pred[1024]{0:T(1024)(128)(4,1)} %fusion.79, bf16[1024,4,128,1]{2,1,0,3:T(4,128)(2,1)} %bitcast.168, bf16[32,4,8,128]{3,2,1,0:T(8,128)(2,1)S(1)} %pad_maximum_fusion), kind=kOutput, calls=%fused_computation.6 | convolution fusion | flops 271580160 | bytes 5510144 | tf_op jit(solution)/shard_map/while/body/eval_jaxpr/nkgd,mkd->kgnm/dot_general | solution.py:105
  103.5 1.4 fusion.91
  107.0 3.2 %fusion.1 = f32[4,8,32]{1,2,0:T(8,128)S(1)} fusion(f32[4,32,8,1024]{3,2,1,0:T(8,128)} %get-tuple-element.67, f32[4,8,32]{1,2,0:T(8,128)S(1)} %copy.204, pred[1024]{0:T(1024)(128)(4,1)} %fusion.79), kind=kLoop, calls=%fused_computation.11 | loop fusion | flops 4193280 | bytes 4203520 | tf_op jit(solution)/shard_map/while/body/eval_jaxpr/reduce_sum | solution.py:129
  116.0 3.7 %fusion.12 = f32[32,4,8,128]{3,2,0,1:T(8,128)S(1)} fusion(f32[4,32,8,1024]{3,2,1,0:T(8,128)} %get-tuple-element.67, f32[4,8,32]{1,2,0:T(8,128)S(1)} %copy.206, f32[4,8,32]{1,2,0:T(8,128)} %copy-done.4, pred[1024]{0:T(1024)(128)(4,1)} %fusion.79, bf16[1024,4,128,1]{2,1,0,3:T(4,128)(2,1)} %bitcast.174), kind=kOutput, calls=%fused_computation.20 | convolution fusion | flops 273678336 | bytes 5776384 | tf_op jit(solution)/shard_map/while/body/eval_jaxpr/kgnm,mkd->nkgd/dot_general | solution.py:136
  120.4 16.2 %all_to_all.55 = bf16[32,32,128]{2,0,1:T(8,128)(2,1)S(1)} all-to-all(bf16[32,32,128]{2,0,1:T(8,128)(2,1)S(1)} %copy.212), channel_id=1, replica_groups=mesh['group'=8,'tensor'=32] {'tensor'}, dimensions={1} | all-to-all | bytes 524288 | tf_op jit(solution)/shard_map/all_to_all | solution.py:212
  136.6 3.2 %convolution_convert_fusion = bf16[1024,2048]{1,0:T(8,128)(2,1)} fusion(bf16[1024,128]{1,0:T(8,128)(2,1)S(1)} %bitcast.169, bf16[128,2048]{1,0:T(8,128)(2,1)S(1)} %copy-done.3), kind=kOutput, calls=%fused_computation.10 | convolution fusion | flops 538968064 | bytes 4980736 | tf_op jit(solution)/shard_map/dot_general | solution.py:214
  142.3 83.0 %reduce-scatter.2.cloned.1.call-done = bf16[32,2048]{1,0:T(8,128)(2,1)} async-done(((bf16[1024,2048]{1,0:T(8,128)(2,1)}), bf16[32,2048]{1,0:T(8,128)(2,1)}) %reduce-scatter.2.cloned.1.call-update) | async-done | bytes 131088 | tf_op jit(solution)/shard_map/reduce_scatter | solution.py:213
  227.4 1.4 gather_fusion
  228.9 1.8 reshape.308
  230.7 7.3 %all-to-all-start.3 = ((bf16[32,2,2048]{2,1,0:T(2,128)(2,1)}), bf16[32,2,2048]{2,1,0:T(2,128)(2,1)}, u32[]{:S(2)}, u32[]{:S(2)}) async-start(bf16[32,2,2048]{2,1,0:T(2,128)(2,1)} %reshape.308), calls=%async_computation.4 | async-start | bytes 524288 | tf_op jit(solution)/shard_map/all_to_all | solution.py:228
  240.7 6.3 %all-to-all-done.3 = bf16[32,2,2048]{2,1,0:T(2,128)(2,1)} async-done(((bf16[32,2,2048]{2,1,0:T(2,128)(2,1)}), bf16[32,2,2048]{2,1,0:T(2,128)(2,1)}, u32[]{:S(2)}, u32[]{:S(2)}) %all-to-all-start.3) | async-done | bytes 262176 | tf_op jit(solution)/shard_map/all_to_all | solution.py:228
  247.1 3.7 %fusion.18 = f32[32,1,2,768]{3,0,2,1:T(8,128)} fusion(bf16[1,768,2048]{2,1,0:T(8,128)(2,1)} %param.30, bf16[32,2,2048]{2,1,0:T(2,128)(2,1)} %all-to-all-done.3), kind=kOutput, calls=%fused_computation.30 | convolution fusion | flops 201326592 | bytes 3604480 | tf_op jit(solution)/shard_map/spcd,pfd->spcf/dot_general | solution.py:231
  250.8 4.8 %fusion.8 = bf16[32,2,2048]{2,0,1:T(8,128)(2,1)} fusion(bf16[1,768,2048]{2,1,0:T(8,128)(2,1)S(1)} %copy-done, bf16[1,768,2048]{2,1,0:T(8,128)(2,1)} %param.31, bf16[32,2,2048]{2,1,0:T(2,128)(2,1)} %all-to-all-done.3, f32[32,1,2,768]{3,0,2,1:T(8,128)} %fusion.18), kind=kOutput, calls=%fused_computation.18 | convolution fusion | flops 403079168 | bytes 7012352 | tf_op jit(solution)/shard_map/spcf,pfd->spcd/dot_general | solution.py:234
  255.6 1.9 copy.218
  257.5 4.4 %all-to-all-start.4 = ((bf16[32,2,2048]{2,1,0:T(2,128)(2,1)}), bf16[32,2,2048]{2,1,0:T(2,128)(2,1)}, u32[]{:S(2)}, u32[]{:S(2)}) async-start(bf16[32,2,2048]{2,1,0:T(2,128)(2,1)} %copy.218), calls=%async_computation.5 | async-start | bytes 524288 | tf_op jit(solution)/shard_map/all_to_all | solution.py:236
  262.9 8.1 %all-to-all-done.4 = bf16[32,2,2048]{2,1,0:T(2,128)(2,1)} async-done(((bf16[32,2,2048]{2,1,0:T(2,128)(2,1)}), bf16[32,2,2048]{2,1,0:T(2,128)(2,1)}, u32[]{:S(2)}, u32[]{:S(2)}) %all-to-all-start.4) | async-done | bytes 262176 | tf_op jit(solution)/shard_map/all_to_all | solution.py:236
  271.0 2.0 convert_multiply_fusion
  273.0 2.2 reshape.325
  275.2 2.0 scatter_fusion
  (114 shorter events, 33.6 us)
Async XLA Ops:
  6.5 244.3 %copy-start = (bf16[1,768,2048]{2,1,0:T(8,128)(2,1)S(1)}, bf16[1,768,2048]{2,1,0:T(8,128)(2,1)}, u32[]{:S(2)}) copy-start(bf16[1,768,2048]{2,1,0:T(8,128)(2,1)} %param.32) | copy-start | bytes 9437188
  6.5 11.5 %copy-start.16 = (s32[1,8]{1,0:T(1,128)S(1)}, s32[1,8]{1,0:T(1,128)}, u32[]{:S(2)}) copy-start(s32[1,8]{1,0:T(1,128)} %param.37) | copy-start | bytes 100
  6.5 58.7 %copy-start.6 = (bf16[32,2048]{1,0:T(8,128)(2,1)S(1)}, bf16[32,2048]{1,0:T(8,128)(2,1)}, u32[]{:S(2)}) copy-start(bf16[32,2048]{1,0:T(8,128)(2,1)} %param.25) | copy-start | bytes 393220
  6.5 58.7 %all-gather.2.cloned.1.call-start = ((), (), s32[]{:S(2)}) async-start(), calls=%async_computation.6 | async-start | bytes 4325376 | tf_op jit(solution)/shard_map/all_gather | solution.py:184
  69.8 12.6 %all-to-all-start.1 = ((bf16[32,2,512]{2,1,0:T(2,128)(2,1)}), bf16[32,2,512]{2,1,0:T(2,128)(2,1)S(1)}, u32[]{:S(2)}, u32[]{:S(2)}) async-start(bf16[32,2,512]{2,1,0:T(2,128)(2,1)} %reshape.354), calls=%async_computation.1 | async-start | bytes 131072 | tf_op jit(solution)/shard_map/all_to_all | solution.py:191
  82.5 14.2 %all-to-all-start = ((bf16[32,32,128]{2,1,0:T(8,128)(2,1)}), bf16[32,32,128]{2,1,0:T(8,128)(2,1)S(1)}, u32[]{:S(2)}, u32[]{:S(2)}) async-start(bf16[32,32,128]{2,1,0:T(8,128)(2,1)} %bitcast.176), calls=%async_computation | async-start | bytes 524288 | tf_op jit(solution)/shard_map/all_to_all | solution.py:190
  86.8 138.5 %reduce-scatter.2.cloned.1.call-start = ((), (), s32[]{:S(2)}) async-start(), calls=%async_computation.7 | async-start | bytes 4325376 | tf_op jit(solution)/shard_map/reduce_scatter | solution.py:213
  98.7 4.8 %copy-start.10 = (pred[32,32]{0,1:T(8,128)(4,1)S(1)}, pred[32,32]{0,1:T(8,128)(4,1)}, u32[]{:S(2)}) copy-start(pred[32,32]{0,1:T(8,128)(4,1)} %copy.198) | copy-start | bytes 3076
  98.7 6.2 %copy-start.9 = (bf16[8,512]{1,0:T(8,128)(2,1)S(1)}, bf16[8,512]{1,0:T(8,128)(2,1)}, u32[]{:S(2)}) copy-start(bf16[8,512]{1,0:T(8,128)(2,1)} %gather_fusion.2) | copy-start | bytes 24580
  98.7 6.2 %copy-start.12 = (pred[8]{0:T(512)(128)(4,1)S(1)}, pred[8]{0:T(512)(128)(4,1)}, u32[]{:S(2)}) copy-start(pred[8]{0:T(512)(128)(4,1)} %get-tuple-element.32) | copy-start | bytes 28
  106.9 4.5 %copy-start.4 = (f32[4,8,32]{1,2,0:T(8,128)}, f32[4,8,32]{1,2,0:T(8,128)S(1)}, u32[]{:S(2)}) copy-start(f32[4,8,32]{1,2,0:T(8,128)S(1)} %copy.204) | copy-start | bytes 12292
  111.4 1.2 copy-start.5
  116.0 3.7 %copy-start.8 = (bf16[8,512]{1,0:T(8,128)(2,1)S(1)}, bf16[8,512]{1,0:T(8,128)(2,1)}, u32[]{:S(2)}) copy-start(bf16[8,512]{1,0:T(8,128)(2,1)} %gather_fusion.3) | copy-start | bytes 24580
  116.0 3.7 %copy-start.13 = (pred[8]{0:T(512)(128)(4,1)S(1)}, pred[8]{0:T(512)(128)(4,1)}, u32[]{:S(2)}) copy-start(pred[8]{0:T(512)(128)(4,1)} %get-tuple-element.32) | copy-start | bytes 28
  116.0 4.0 %copy-start.2 = (bf16[4,8,32,32]{3,1,2,0:T(8,128)(2,1)S(1)}, bf16[4,8,32,32]{3,1,2,0:T(8,128)(2,1)}, u32[]{:S(2)}) copy-start(bf16[4,8,32,32]{3,1,2,0:T(8,128)(2,1)} %copy.210) | copy-start | bytes 196612
  116.0 4.0 %copy-start.7 = (bf16[32,4,128]{2,1,0:T(4,128)(2,1)S(1)}, bf16[32,4,128]{2,1,0:T(4,128)(2,1)}, u32[]{:S(2)}) copy-start(bf16[32,4,128]{2,1,0:T(4,128)(2,1)} %reshape.282) | copy-start | bytes 98308
  119.7 16.9 %copy-start.3 = (bf16[128,2048]{1,0:T(8,128)(2,1)S(1)}, bf16[128,2048]{1,0:T(8,128)(2,1)}, u32[]{:S(2)}) copy-start(bf16[128,2048]{1,0:T(8,128)(2,1)} %param.28) | copy-start | bytes 1572868
  139.8 85.5 %copy-start.1 = (bf16[32,2048]{1,0:T(8,128)(2,1)S(1)}, bf16[32,2048]{1,0:T(8,128)(2,1)}, u32[]{:S(2)}) copy-start(bf16[32,2048]{1,0:T(8,128)(2,1)} %param.22) | copy-start | bytes 393220
  139.8 86.6 %copy-start.11 = (f32[2048]{0:T(1024)S(1)}, f32[2048]{0:T(1024)}, u32[]{:S(2)}) copy-start(f32[2048]{0:T(1024)} %param.29) | copy-start | bytes 24580
  141.6 84.8 %copy-start.15 = (s32[32,32]{0,1:T(8,128)}, s32[32,32]{0,1:T(8,128)S(1)}, u32[]{:S(2)}) copy-start(s32[32,32]{0,1:T(8,128)S(1)} %get-tuple-element.31) | copy-start | bytes 12292
  230.7 16.4 %all-to-all-start.3 = ((bf16[32,2,2048]{2,1,0:T(2,128)(2,1)}), bf16[32,2,2048]{2,1,0:T(2,128)(2,1)}, u32[]{:S(2)}, u32[]{:S(2)}) async-start(bf16[32,2,2048]{2,1,0:T(2,128)(2,1)} %reshape.308), calls=%async_computation.4 | async-start | bytes 524288 | tf_op jit(solution)/shard_map/all_to_all | solution.py:228
  250.8 11.8 %copy-start.14 = (s32[32,2]{0,1:T(2,128)S(1)}, s32[32,2]{0,1:T(2,128)}, u32[]{:S(2)}) copy-start(s32[32,2]{0,1:T(2,128)} %get-tuple-element.59) | copy-start | bytes 772
  257.5 13.5 %all-to-all-start.4 = ((bf16[32,2,2048]{2,1,0:T(2,128)(2,1)}), bf16[32,2,2048]{2,1,0:T(2,128)(2,1)}, u32[]{:S(2)}, u32[]{:S(2)}) async-start(bf16[32,2,2048]{2,1,0:T(2,128)(2,1)} %copy.218), calls=%async_computation.5 | async-start | bytes 524288 | tf_op jit(solution)/shard_map/all_to_all | solution.py:236
Sparse Core Ops, SparseCore 0:
  9.9 55.2 all-gather.1
  139.9 85.3 reduce-scatter.1
where the time goes:
time: 286 us; the launch traced here: 285 us
  waiting for transfers between devices  141 us (49%)
  local copies, waits for them, and re-layouts  32.4 us (11%)
  matrix products  31.7 us (11%)
  other arithmetic  26.5 us (9%)
  starting transfers between devices  21.3 us (7%)
  blocking collectives  16.2 us (6%)
  between operations  15.8 us (6%)
    reduce_scatter x1, waiting for transfers between devices, body(): lax.psum_scatter(jnp.dot(attn_heads, w_out, preferred_element_type=jnp.fl...  83 us
    all_gather x1, waiting for transfers between devices, body(): gathered = lax.all_gather(normed_own, 'tensor', axis=0, tiled=True)  40.2 us
    all_to_all x1, blocking collectives, body(): lax.all_to_all(attn_own, 'tensor', split_axis=1, concat_axis=0, tiled=True)  16.2 us
    all_to_all x1, waiting for transfers between devices, body(): lax.all_to_all(result.astype(jnp.bfloat16), 'tensor', split_axis=0, conca...  8.13 us
    all_to_all x1, starting transfers between devices, body(): lax.all_to_all(send_rows, 'tensor', split_axis=0, concat_axis=0, tiled=True)  7.32 us
    all_to_all x1, waiting for transfers between devices, body(): lax.all_to_all(send_rows, 'tensor', split_axis=0, concat_axis=0, tiled=True)  6.34 us
  transfers between devices with their start and end apart: 6, of which 5 were waited for; matrix products, arithmetic and copies ran while one was open for 12% of the time, Pallas kernels for 0%

commit v1 on v0

v1 whole, which is shorter than its diff:
```python
import functools
import math

import jax
import jax.numpy as jnp
import numpy as np
from jax import lax
from jax.experimental import pallas as pl
from jax.experimental.pallas import tpu as pltpu
from jax.sharding import PartitionSpec as P

SINK = 4
WIN = 512
EPSILON = 1e-06
NEG_FILL = -1e30
ROPE_BASE = 1000000.0

N = 32
TOKS = 32
D = 2048
HD = 128
FF = 768
CACHE = 1024
SCALE = HD**-0.5
LOG2E = math.log2(math.e)

BF = jnp.bfloat16
F32 = jnp.float32
MESH = pl.DeviceIdType.MESH
NT = (((1,), (1,)), ((), ()))
TN = (((0,), (0,)), ((), ()))


def dot(a, b, dims=(((1,), (0,)), ((), ()))):
    return lax.dot_general(a, b, dims, preferred_element_type=F32)


def layer_kernel(
    freq_ref, attn_gain, query_gain, key_gain, ffn_gain, parents, prefix, accepted, path, kind,
    res_hbm, wq_hbm, wkv_hbm, wo_hbm, wg_hbm, wu_hbm, wd_hbm, kc_hbm, vc_hbm, ids_hbm, gates_hbm,
    out_ref,
    res, wq, wkv, wo, wg, wu, wd, kc, vc, ids, gates,
    ag, qsend, qrecv, asend, ain,
    part, s1, r1, s2, r2, u1, v1, u2, v2, rsum,
    fs, xs, dsend, drecv, ysend, yrecv, sel_ref, comb_ref, cos_ref, sin_ref, allow_ref,
    lsem, wsend, wrecv, gs, ga, gh, gb, gbh, hs, qs, qr, asem, ar,
    t1s, t1r, t2s, t2r, p1s, p1r, p2s, p2r, ds, dr, ys, yr,
):
    t = lax.axis_index("tensor")
    core = lax.rem(t, 2)
    chip = t // 2
    cx = chip // 4
    cy = lax.rem(chip, 4)
    a = cx * (1 - core) + cy * core
    b = cy * (1 - core) + cx * core
    step_a = 8 - 6 * core
    step_b = 2 + 6 * core

    def dev(a_, b_):
        return a_ * step_a + b_ * step_b + core

    def ring(v, k):
        return lax.rem(v + k, 4)

    def remote(src, dst, ssem, rsem, to):
        return pltpu.make_async_remote_copy(
            src_ref=src, dst_ref=dst, send_sem=ssem, recv_sem=rsem,
            device_id={"tensor": to}, device_id_type=MESH,
        )

    def await_bytes(ref, sem):
        pltpu.make_async_copy(ref, ref, sem).wait()

    load_res = pltpu.make_async_copy(res_hbm, res, lsem.at[0])
    load_res.start()
    wkv[...] = jnp.zeros_like(wkv)
    lane0 = pl.multiple_of(core * HD, HD)
    kv_row = pl.multiple_of(lax.rem(chip, 2) * 64 + core * 32, 32)
    lane_win = pl.multiple_of((t // 4) * HD, HD)
    loads = [
        pltpu.make_async_copy(wq_hbm, wq.at[:, pl.ds(lane0, HD)], lsem.at[1]),
        pltpu.make_async_copy(wkv_hbm, wkv.at[pl.ds(kv_row, 32)], lsem.at[2]),
        pltpu.make_async_copy(ids_hbm.at[:, pl.ds(lane_win, HD)], ids, lsem.at[3]),
        pltpu.make_async_copy(gates_hbm.at[:, pl.ds(lane_win, HD)], gates, lsem.at[4]),
        pltpu.make_async_copy(wo_hbm, wo.at[pl.ds(lane0, HD)], lsem.at[5]),
        pltpu.make_async_copy(kc_hbm.at[0], kc, lsem.at[6]),
        pltpu.make_async_copy(vc_hbm.at[0], vc, lsem.at[7]),
        pltpu.make_async_copy(wg_hbm.at[0], wg, lsem.at[8]),
        pltpu.make_async_copy(wu_hbm.at[0], wu, lsem.at[9]),
        pltpu.make_async_copy(wd_hbm.at[0], wd, lsem.at[10]),
    ]
    for load in loads:
        load.start()

    barrier = pltpu.get_barrier_semaphore()

    def greet(k, carry):
        pl.semaphore_signal(
            barrier, inc=1, device_id={"tensor": lax.rem(t + k, N)}, device_id_type=MESH
        )
        return carry

    lax.fori_loop(1, N, greet, 0)

    load_res.wait()
    own = b * 4 + a
    xv = res[...].astype(F32)
    inv = lax.rsqrt(jnp.mean(xv * xv, axis=-1, keepdims=True) + EPSILON)
    ag[own] = (xv * inv * attn_gain[...][None, :]).astype(BF)

    pl.semaphore_wait(barrier, N - 1)

    up_a, down_a = dev(ring(a, 1), b), dev(ring(a, 3), b)
    up_b, down_b = dev(a, ring(b, 1)), dev(a, ring(b, 3))

    def blk(a_, b_):
        return ag.at[b_ * 4 + a_]

    def half(a_, b_, h):
        return ag.at[b_ * 4 + a_, pl.ds(16 * h, 16)]

    sends = []

    def go(copy):
        copy.start()
        sends.append(copy)

    def spread_b(j, a_):
        go(remote(blk(a_, b), blk(a_, b), gs.at[2 + 2 * j], gb.at[j, 0], up_b))
        go(remote(blk(a_, b), blk(a_, b), gs.at[3 + 2 * j], gb.at[j, 1], down_b))

    go(remote(blk(a, b), blk(a, b), gs.at[0], ga.at[0], up_a))
    go(remote(blk(a, b), blk(a, b), gs.at[1], ga.at[1], down_a))
    spread_b(0, a)

    sibling = t + 1 - 2 * core
    go(remote(wq_hbm, wq.at[:, pl.ds(lane0, HD)], wsend.at[0], wrecv.at[0], sibling))
    go(remote(wkv_hbm, wkv.at[pl.ds(kv_row, 32)], wsend.at[1], wrecv.at[1], sibling))
    go(remote(wo_hbm, wo.at[pl.ds(lane0, HD)], wsend.at[2], wrecv.at[2], sibling))

    am, ap, af = ring(a, 3), ring(a, 1), ring(a, 2)
    bm, bp, bf = ring(b, 3), ring(b, 1), ring(b, 2)

    await_bytes(blk(am, b), ga.at[0])
    go(remote(half(am, b, 0), half(am, b, 0), hs.at[0], gh.at[0], up_a))
    spread_b(1, am)
    await_bytes(blk(ap, b), ga.at[1])
    go(remote(half(ap, b, 1), half(ap, b, 1), hs.at[1], gh.at[1], down_a))
    spread_b(2, ap)

    def relay_b(j, a_):
        await_bytes(blk(a_, bm), gb.at[j, 0])
        go(remote(half(a_, bm, 0), half(a_, bm, 0), hs.at[2 + 2 * j], gbh.at[j, 0], up_b))
        await_bytes(blk(a_, bp), gb.at[j, 1])
        go(remote(half(a_, bp, 1), half(a_, bp, 1), hs.at[3 + 2 * j], gbh.at[j, 1], down_b))

    relay_b(0, a)
    await_bytes(half(af, b, 0), gh.at[0])
    await_bytes(half(af, b, 1), gh.at[1])
    spread_b(3, af)

    for load in loads[:2]:
        load.wait()
    other_lane = pl.multiple_of(HD - core * HD, HD)
    other_row = pl.multiple_of(lax.rem(chip, 2) * 64 + 32 - core * 32, 32)
    await_bytes(wq.at[:, pl.ds(other_lane, HD)], wrecv.at[0])
    await_bytes(wkv.at[pl.ds(other_row, 32)], wrecv.at[1])

    def project(b_):
        rows = ag[pl.ds(b_ * 4, 4)].reshape(4 * TOKS, D)
        q = dot(rows, wq[...])
        kv = dot(rows, wkv[...], NT)
        qsend[pl.ds(b_ * 4, 4), :, 0 : 2 * HD] = q.astype(BF).reshape(4, TOKS, 2 * HD)
        qsend[pl.ds(b_ * 4, 4), :, 2 * HD :] = kv.astype(BF).reshape(4, TOKS, HD)

    def post_queries(b_, first):
        for k in range(first, 4):
            a_ = ring(a, k)
            copy = remote(
                qsend.at[b_ * 4 + a_], qrecv.at[chip], qs, qr, dev(a_, b_)
            )
            copy.start()

    project(b)
    qrecv[chip] = qsend[own]
    post_queries(b, 1)

    relay_b(1, am)
    relay_b(2, ap)

    for load in loads[2:4]:
        load.wait()
    line = lax.broadcasted_iota(jnp.int32, (2 * N, TOKS), 0)
    expert = line // 2
    named = jnp.zeros((2 * N, TOKS), F32)
    weight = jnp.zeros((2 * N, TOKS), F32)
    turn_lanes = lax.rem(HD - lax.rem(t, 4) * TOKS, HD)
    idv = pltpu.roll(ids[...], turn_lanes, 1)[:, 0:TOKS]
    gv = pltpu.roll(gates[...], turn_lanes, 1)[:, 0:TOKS]
    for k in range(8):
        hit = jnp.broadcast_to(idv[k : k + 1], (2 * N, TOKS)) == expert
        named = jnp.where(hit, 1.0, named)
        weight = weight + jnp.where(hit, jnp.broadcast_to(gv[k : k + 1], (2 * N, TOKS)), 0.0)
    ri = lax.broadcasted_iota(jnp.int32, (TOKS, TOKS), 0)
    ci = lax.broadcasted_iota(jnp.int32, (TOKS, TOKS), 1)
    before = dot(named.astype(BF), jnp.where(ri < ci, 1.0, 0.0).astype(BF))
    turn = lax.rem(line, 2).astype(F32)
    taken = (named > 0.5) & (jnp.abs(before - turn) < 0.5)
    sel_ref[...] = jnp.where(taken, 1.0, 0.0).astype(BF)
    comb_ref[...] = jnp.where(taken, weight, 0.0)

    link = jnp.where((ri == jnp.broadcast_to(parents[...], (TOKS, TOKS))) | (ri == ci), 1.0, 0.0)
    for unused in range(5):
        link = jnp.minimum(dot(link.astype(BF), link.astype(BF)), 1.0)
    eye = jnp.where(ri == ci, 1.0, 0.0).astype(BF)
    reach = dot(link.astype(BF), eye, TN)
    is_tree = kind[0, 0] == 1
    causal = jnp.where(ci <= ri, 1.0, 0.0)
    allowed = jnp.where(is_tree, reach, causal)
    allow_ref[...] = allowed
    depth = jnp.sum(allowed, axis=1, keepdims=True) - 1.0
    total = prefix[0, 0] + accepted[0, 0]
    angle = (total.astype(F32) + depth) * freq_ref[...]
    cos_ref[...] = jnp.cos(angle)
    lane_row = lax.broadcasted_iota(jnp.int32, (TOKS, HD), 1)
    sine = jnp.sin(angle)
    sin_ref[...] = jnp.where(lane_row < HD // 2, -sine, sine)

    relay_b(3, af)
    project(bm)
    post_queries(bm, 0)
    project(bp)
    post_queries(bp, 0)

    for j, a_ in enumerate((a, am, ap, af)):
        await_bytes(half(a_, bf, 0), gbh.at[j, 0])
        await_bytes(half(a_, bf, 1), gbh.at[j, 1])
    project(bf)
    post_queries(bf, 0)

    row = lax.broadcasted_iota(jnp.int32, (1, CACHE), 1)
    seen = (row < prefix[0, 0]) & ((row < SINK) | (row >= total - WIN))
    for m in range(8):
        seen = seen | ((row == prefix[0, 0] + path[0, m]) & (accepted[0, 0] > m))
    for load in loads[5:7]:
        load.wait()
    await_bytes(qrecv.at[pl.ds(0, 15)], qr)

    def rope(v, gain):
        v = v * lax.rsqrt(jnp.mean(v * v, axis=-1, keepdims=True) + EPSILON) * gain
        return (v * cos_ref[...] + pltpu.roll(v, HD // 2, 1) * sin_ref[...]).astype(BF)

    def heads(g, carry):
        qgain = query_gain[...][None, :]
        qg = jnp.concatenate(
            [
                rope(qrecv[4 * g + i, :, HD * j : HD * (j + 1)].astype(F32), qgain)
                for i in range(4)
                for j in range(2)
            ],
            axis=0,
        )
        kraw = qrecv[2 * g, :, 2 * HD :].astype(F32) + qrecv[2 * g + 1, :, 2 * HD :].astype(F32)
        knew = rope(kraw, key_gain[...][None, :])
        vnew = qrecv[8 + 2 * g, :, 2 * HD :] + qrecv[9 + 2 * g, :, 2 * HD :]
        cols = pl.ds(pl.multiple_of(g * HD, HD), HD)
        s_old = dot(qg, kc[:, cols], NT)
        s_new = dot(qg, knew, NT)
        s_old = jnp.where(jnp.broadcast_to(seen, s_old.shape), s_old, NEG_FILL)
        allow = jnp.concatenate([allow_ref[...]] * 8, axis=0)
        s_new = jnp.where(allow > 0.5, s_new, NEG_FILL)
        top = jnp.maximum(
            jnp.max(s_old, axis=-1, keepdims=True), jnp.max(s_new, axis=-1, keepdims=True)
        )
        e_old = jnp.exp2((s_old - top) * (SCALE * LOG2E))
        e_new = jnp.exp2((s_new - top) * (SCALE * LOG2E))
        denom = jnp.sum(e_old, axis=-1, keepdims=True) + jnp.sum(e_new, axis=-1, keepdims=True)
        o = dot(e_old.astype(BF), vc[:, cols]) + dot(e_new.astype(BF), vnew)
        o = (o / denom).astype(BF)
        for i in range(4):
            to = 4 * g + i
            for j in range(2):
                r0 = (2 * i + j) * TOKS
                asend[to, :, HD * j : HD * (j + 1)] = o[r0 : r0 + TOKS]

            @pl.when(to != chip)
            def _():
                remote(asend.at[to], ain.at[own], asem, ar.at[b], 2 * to + core).start()

        return carry

    lax.fori_loop(0, 4, heads, 0)
    ain[own] = asend[chip]

    loads[4].wait()
    await_bytes(wo.at[pl.ds(other_lane, HD)], wrecv.at[2])
    order = (bf, bp, bm, b)
    for k, b_ in enumerate(order):
        await_bytes(ain.at[pl.ds(b_ * 4, 3 if k == 3 else 4)], ar.at[b_])
        part[k] = dot(ain[pl.ds(b_ * 4, 4)].reshape(4 * TOKS, 2 * HD), wo[...])
        far = pl.multiple_of(af * TOKS, TOKS)
        s1[k, 0] = part[k, pl.ds(far, 16), :].astype(BF)
        go(remote(s1.at[k, 0], r1.at[k, 0], t1s.at[k, 0], t1r.at[k, 0], up_a))
        s1[k, 1] = part[k, pl.ds(far + 16, 16), :].astype(BF)
        go(remote(s1.at[k, 1], r1.at[k, 1], t1s.at[k, 1], t1r.at[k, 1], down_a))
    for k in range(4):
        to_up = pl.multiple_of(ap * TOKS, TOKS)
        await_bytes(r1.at[k, 0], t1r.at[k, 0])
        s2[k, 0, 0:16] = (part[k, pl.ds(to_up, 16), :] + r1[k, 0].astype(F32)).astype(BF)
        s2[k, 0, 16:32] = part[k, pl.ds(to_up + 16, 16), :].astype(BF)
        go(remote(s2.at[k, 0], r2.at[k, 0], t2s.at[k, 0], t2r.at[k, 0], up_a))
        to_down = pl.multiple_of(am * TOKS, TOKS)
        await_bytes(r1.at[k, 1], t1r.at[k, 1])
        s2[k, 1, 0:16] = part[k, pl.ds(to_down, 16), :].astype(BF)
        s2[k, 1, 16:32] = (part[k, pl.ds(to_down + 16, 16), :] + r1[k, 1].astype(F32)).astype(BF)
        go(remote(s2.at[k, 1], r2.at[k, 1], t2s.at[k, 1], t2r.at[k, 1], down_a))
    mine = pl.multiple_of(a * TOKS, TOKS)
    for k in range(4):
        await_bytes(r2.at[k, 0], t2r.at[k, 0])
        await_bytes(r2.at[k, 1], t2r.at[k, 1])
        rs = part[k, pl.ds(mine, TOKS), :] + r2[k, 0].astype(F32) + r2[k, 1].astype(F32)
        if k == 0:
            u1[0] = rs[0:16].astype(BF)
            u1[1] = rs[16:32].astype(BF)
            go(remote(u1.at[0], v1.at[0], p1s.at[0], p1r.at[0], up_b))
            go(remote(u1.at[1], v1.at[1], p1s.at[1], p1r.at[1], down_b))
        elif k == 1:
            await_bytes(v1.at[0], p1r.at[0])
            u2[0, 0:16] = (rs[0:16] + v1[0].astype(F32)).astype(BF)
            u2[0, 16:32] = rs[16:32].astype(BF)
            go(remote(u2.at[0], v2.at[0], p2s.at[0], p2r.at[0], up_b))
        elif k == 2:
            await_bytes(v1.at[1], p1r.at[1])
            u2[1, 0:16] = rs[0:16].astype(BF)
            u2[1, 16:32] = (rs[16:32] + v1[1].astype(F32)).astype(BF)
            go(remote(u2.at[1], v2.at[1], p2s.at[1], p2r.at[1], down_b))
        else:
            rsum[...] = rs
    await_bytes(v2.at[0], p2r.at[0])
    await_bytes(v2.at[1], p2r.at[1])
    hidden = res[...].astype(F32) + (
        rsum[...] + v2[0].astype(F32) + v2[1].astype(F32)
    )
    rsum[...] = hidden
    inv = lax.rsqrt(jnp.mean(hidden * hidden, axis=-1, keepdims=True) + EPSILON)
    normed = (hidden * inv * ffn_gain[...][None, :]).astype(BF)

    picked = dot(sel_ref[...], normed)
    for j in range(16):
        fs[pl.ds(j, 64, stride=16), :] = picked[:, HD * j : HD * (j + 1)]
    dsend[...] = fs[...].astype(BF).reshape(N, 32, HD)

    def post(src, dst, ssem, rsem):
        def one(k, carry):
            to = lax.rem(t + k, N)
            remote(src.at[to], dst.at[t], ssem, rsem, to).start()
            return carry

        lax.fori_loop(1, N, one, 0)

    post(dsend, drecv, ds, dr)
    drecv[t] = dsend[t]
    for load in loads[7:]:
        load.wait()
    await_bytes(drecv.at[pl.ds(0, N - 1)], dr)
    fs[...] = drecv[...].reshape(1024, HD).astype(F32)
    for j in range(16):
        xs[:, HD * j : HD * (j + 1)] = fs[pl.ds(j, 64, stride=16), :].astype(BF)
    gate = dot(xs[...], wg[...], NT)
    up = dot(xs[...], wu[...], NT)
    inner = (gate / (1.0 + jnp.exp(-gate)) * up).astype(BF)
    y = dot(inner, wd[...])
    for j in range(16):
        fs[pl.ds(j, 64, stride=16), :] = y[:, HD * j : HD * (j + 1)]
    ysend[...] = fs[...].astype(BF).reshape(N, 32, HD)
    post(ysend, yrecv, ys, yr)
    yrecv[t] = ysend[t]
    await_bytes(yrecv.at[pl.ds(0, N - 1)], yr)
    fs[...] = yrecv[...].reshape(1024, HD).astype(F32)
    comb = comb_ref[...]
    comb_hi = comb.astype(BF)
    comb_lo = (comb - comb_hi.astype(F32)).astype(BF)
    for j in range(16):
        yj = fs[pl.ds(j, 64, stride=16), :].astype(BF)
        moe = dot(comb_hi, yj, TN) + dot(comb_lo, yj, TN)
        cols = slice(HD * j, HD * (j + 1))
        out_ref[:, cols] = (rsum[:, cols] + moe).astype(BF)

    for copy in sends:
        copy.wait_send()
    await_bytes(qsend.at[pl.ds(0, 15)], qs)
    await_bytes(asend.at[pl.ds(0, 15)], asem)
    await_bytes(dsend.at[pl.ds(0, N - 1)], ds)
    await_bytes(ysend.at[pl.ds(0, N - 1)], ys)


def body(
    residual_in, attn_gain, w_query, w_keyval, query_gain, key_gain, w_out, ffn_gain,
    w_gate, w_up, w_down, key_cache, value_cache, prefix_lens, accepted, accept_path,
    parents, slot_kinds, expert_ids, gate_probs,
):
    half = np.arange(HD // 2, dtype=np.float64)
    freq = np.exp(-(2.0 * half / HD) * math.log(ROPE_BASE)).astype(np.float32)
    freq = jnp.asarray(np.concatenate([freq, freq])[None, :])
    vmem = pl.BlockSpec(memory_space=pltpu.VMEM)
    smem = pl.BlockSpec(memory_space=pltpu.SMEM)
    hbm = pl.BlockSpec(memory_space=pltpu.HBM)
    dma = pltpu.SemaphoreType.DMA
    vm = pltpu.VMEM
    return pl.pallas_call(
        layer_kernel,
        out_shape=jax.ShapeDtypeStruct((TOKS, D), BF),
        in_specs=[vmem] * 6 + [smem] * 4 + [hbm] * 11,
        out_specs=vmem,
        scratch_shapes=[
            vm((TOKS, D), BF),
            vm((D, 2 * HD), BF),
            vm((HD, D), BF),
            vm((2 * HD, D), BF),
            vm((FF, D), BF),
            vm((FF, D), BF),
            vm((FF, D), BF),
            vm((CACHE, 4 * HD), BF),
            vm((CACHE, 4 * HD), BF),
            vm((8, HD), jnp.int32),
            vm((8, HD), F32),
            vm((16, TOKS, D), BF),
            vm((16, TOKS, 3 * HD), BF),
            vm((16, TOKS, 3 * HD), BF),
            vm((16, TOKS, 2 * HD), BF),
            vm((16, TOKS, 2 * HD), BF),
            vm((4, 4 * TOKS, D), F32),
            vm((4, 2, 16, D), BF),
            vm((4, 2, 16, D), BF),
            vm((4, 2, TOKS, D), BF),
            vm((4, 2, TOKS, D), BF),
            vm((2, 16, D), BF),
            vm((2, 16, D), BF),
            vm((2, TOKS, D), BF),
            vm((2, TOKS, D), BF),
            vm((TOKS, D), F32),
            vm((1024, HD), F32),
            vm((2 * N, D), BF),
            vm((N, 32, HD), BF),
            vm((N, 32, HD), BF),
            vm((N, 32, HD), BF),
            vm((N, 32, HD), BF),
            vm((2 * N, TOKS), BF),
            vm((2 * N, TOKS), F32),
            vm((TOKS, HD), F32),
            vm((TOKS, HD), F32),
            vm((TOKS, TOKS), F32),
            dma((11,)),
            dma((3,)), dma((3,)),
            dma((10,)),
            dma((2,)), dma((2,)),
            dma((4, 2)), dma((4, 2)),
            dma((10,)),
            dma(()), dma(()),
            dma(()), dma((4,)),
            dma((4, 2)), dma((4, 2)), dma((4, 2)), dma((4, 2)),
            dma((2,)), dma((2,)), dma((2,)), dma((2,)),
            dma(()), dma(()), dma(()), dma(()),
        ],
        compiler_params=pltpu.CompilerParams(
            collective_id=0, has_side_effects=True, vmem_limit_bytes=56 * 1024 * 1024
        ),
        name="layer",
    )(
        freq, attn_gain, query_gain, key_gain, ffn_gain, parents,
        prefix_lens[None], accepted[None], accept_path, slot_kinds[None],
        residual_in, w_query, w_keyval, w_out, w_gate, w_up, w_down,
        key_cache, value_cache, expert_ids.T, gate_probs.T,
    )


def solution(mesh):
    in_specs = (
        P(("group", "tensor"), None),
        P(),
        P(None, "tensor"),
        P("tensor", None),
        P(),
        P(),
        P("tensor", None),
        P(),
        P("tensor", None, None),
        P("tensor", None, None),
        P("tensor", None, None),
        P(("group", "tensor"), None, None),
        P(("group", "tensor"), None, None),
        P(("group", "tensor")),
        P(("group", "tensor")),
        P(("group", "tensor"), None),
        P(("group", "tensor"), None),
        P(("group", "tensor")),
        P("group", None),
        P("group", None),
    )
    out_specs = P(("group", "tensor"), None)
    return jax.shard_map(body, mesh=mesh, in_specs=in_specs, out_specs=out_specs, check_vma=False)
```

time: 286 us -> 81.6 us (0.29)
  waiting for transfers between devices: 141 us -> 0 us
  Pallas kernels: 0 us -> 77.9 us
  matrix products: 31.7 us -> 0 us
  local copies, waits for them, and re-layouts: 32.4 us -> 1.57 us
  other arithmetic: 26.5 us -> 0 us
  starting transfers between devices: 21.3 us -> 0 us
  blocking collectives: 16.2 us -> 0 us
  between operations: 15.8 us -> 1.95 us
    reduce_scatter x1 -> x0, waiting for transfers between devices: 83 us -> none  [body(): lax.psum_scatter(jnp.dot(attn_heads, w_out, preferred_element_type=jnp.fl...]
    pallas_call x0 -> x1, Pallas kernels: none -> 77.9 us  [body(): pl.pallas_call(layer_kernel, out_shape=jax.ShapeDtypeStruct((TOKS, D), BF...]
    all_gather x1 -> x0, waiting for transfers between devices: 40.2 us -> none  [body(): gathered = lax.all_gather(normed_own, 'tensor', axis=0, tiled=True)]
    dot_general x16 -> x0, matrix products: 31.7 us -> none  [the longest x1 4.76 us: body(): jnp.einsum('spcf,pfd->spcd', inner_act, w_down, preferred_element_type=jn...]
    all_to_all x4 -> x0, starting transfers between devices: 21.2 us -> none  [the longest x1 7.32 us: body(): lax.all_to_all(send_rows, 'tensor', split_axis=0, concat_axis=0, tiled=True)]
    all_to_all x4 -> x0, waiting for transfers between devices: 17.6 us -> none  [the longest x1 8.13 us: body(): lax.all_to_all(result.astype(jnp.bfloat16), 'tensor', split_axis=0, conca...]
    all_to_all x1 -> x0, blocking collectives: 16.2 us -> none  [body(): lax.all_to_all(attn_own, 'tensor', split_axis=1, concat_axis=0, tiled=True)]
    gather x9 -> x0, local copies, waits for them, and re-layouts: 9.47 us -> none  [the longest x2 3.27 us: body(): send_rows = normed_ffn[chosen]]
  transfers between devices with their start and end apart: 6 -> 0, of which waited for: 5 -> 0; matrix products, arithmetic and copies ran while one was open for 12% -> 0% of each run, Pallas kernels for 0% -> 0%
where the time goes in v1:
time: 81.6 us; the launch traced here: 81.4 us
  Pallas kernels  77.9 us (95%)
  between operations  1.95 us (2%)
  local copies, waits for them, and re-layouts  1.57 us (2%)
    pallas_call x1, Pallas kernels, body(): pl.pallas_call(layer_kernel, out_shape=jax.ShapeDtypeStruct((TOKS, D), BF...  77.9 us

profile of v1, /device:TPU:1, one launch (start us, length us, event | category | flops | bytes accessed | tf_op | source)
XLA Modules:
  0.0 81.4 jit_solution(10806607628968960583)
XLA Ops:
  1.9 77.9 %layer.1 = bf16[32,2048]{1,0:T(8,128)(2,1)} custom-call(f32[1,128]{1,0:T(1,128)} %constant.2.clone.freq_ref, f32[2048]{0:T(1024)} %attn_gain.1, f32[128]{0:T(128)} %query_gain.1, f32[128]{0:T(128)} %key_gain.1, f32[2048]{0:T(1024)} %ffn_gain.1, s32[1,32]{1,0:T(1,128)} %parents.1, s32[1,1]{1,0:T(1,128)} %bitcast.5.prefix, s32[1,1]{1,0:T(1,128)} %bitcast.6.accepted, ...), custom_call_target="tpu_custom_call" | custom-call | tf_op jit(solution)/shard_map/layer/pallas_call | solution.py:410
  79.8 1.6 %copy.26 = bf16[32,2048]{1,0:T(8,128)(2,1)} copy(bf16[32,2048]{1,0:T(8,128)(2,1)} %layer.1) | data formatting | bytes 262144

commit v2 on v1

--- a/solution.py
+++ b/solution.py
@@ -27,6 +27,10 @@
 BF = jnp.bfloat16
 F32 = jnp.float32
 MESH = pl.DeviceIdType.MESH
+FAR_FIRST = sorted(
+    ((i, j) for i in range(4) for j in range(4)),
+    key=lambda ij: -(min(ij[0], 4 - ij[0]) + min(ij[1], 4 - ij[1])),
+)
 NT = (((1,), (1,)), ((), ()))
 TN = (((0,), (0,)), ((), ()))
 
@@ -36,14 +40,15 @@
 
 
 def layer_kernel(
-    freq_ref, attn_gain, query_gain, key_gain, ffn_gain, parents, prefix, accepted, path, kind,
+    freq_hbm, again_hbm, qgain_hbm, kgain_hbm, fgain_hbm, par_hbm, prefix_hbm, acc_hbm, path_hbm, kind_hbm,
     res_hbm, wq_hbm, wkv_hbm, wo_hbm, wg_hbm, wu_hbm, wd_hbm, kc_hbm, vc_hbm, ids_hbm, gates_hbm,
     out_ref,
+    freq_ref, attn_gain, query_gain, key_gain, ffn_gain, parents, prefix, accepted, path, kind,
     res, wq, wkv, wo, wg, wu, wd, kc, vc, ids, gates,
     ag, qsend, qrecv, asend, ain,
     part, s1, r1, s2, r2, u1, v1, u2, v2, rsum,
     fs, xs, dsend, drecv, ysend, yrecv, sel_ref, comb_ref, cos_ref, sin_ref, allow_ref,
-    lsem, wsend, wrecv, gs, ga, gh, gb, gbh, hs, qs, qr, asem, ar,
+    lsem, isem, meet, wsend, wrecv, gs, ga, gh, gb, gbh, hs, qs, qr, asem, ar,
     t1s, t1r, t2s, t2r, p1s, p1r, p2s, p2r, ds, dr, ys, yr,
 ):
     t = lax.axis_index("tensor")
@@ -73,6 +78,17 @@
 
     load_res = pltpu.make_async_copy(res_hbm, res, lsem.at[0])
     load_res.start()
+    small = [
+        pltpu.make_async_copy(src, dst, isem.at[i])
+        for i, (src, dst) in enumerate(
+            (
+                (again_hbm, attn_gain), (freq_hbm, freq_ref), (qgain_hbm, query_gain),
+                (kgain_hbm, key_gain), (fgain_hbm, ffn_gain), (par_hbm, parents),
+                (prefix_hbm, prefix), (acc_hbm, accepted), (path_hbm, path), (kind_hbm, kind),
+            )
+        )
+    ]
+    small[0].start()
     wkv[...] = jnp.zeros_like(wkv)
     lane0 = pl.multiple_of(core * HD, HD)
     kv_row = pl.multiple_of(lax.rem(chip, 2) * 64 + core * 32, 32)
@@ -89,26 +105,24 @@
         pltpu.make_async_copy(wu_hbm.at[0], wu, lsem.at[9]),
         pltpu.make_async_copy(wd_hbm.at[0], wd, lsem.at[10]),
     ]
-    for load in loads:
+    for load in loads[:2] + small[1:] + loads[2:]:
         load.start()
 
     barrier = pltpu.get_barrier_semaphore()
 
-    def greet(k, carry):
-        pl.semaphore_signal(
-            barrier, inc=1, device_id={"tensor": lax.rem(t + k, N)}, device_id_type=MESH
-        )
-        return carry
-
-    lax.fori_loop(1, N, greet, 0)
+    sibling = t + 1 - 2 * core
+    line = [dev(ring(a, k), b) for k in (1, 2, 3)] + [dev(a, ring(b, k)) for k in (1, 2, 3)]
+    for to in line + [sibling]:
+        pl.semaphore_signal(barrier, inc=1, device_id={"tensor": to}, device_id_type=MESH)
 
     load_res.wait()
+    small[0].wait()
     own = b * 4 + a
     xv = res[...].astype(F32)
     inv = lax.rsqrt(jnp.mean(xv * xv, axis=-1, keepdims=True) + EPSILON)
     ag[own] = (xv * inv * attn_gain[...][None, :]).astype(BF)
 
-    pl.semaphore_wait(barrier, N - 1)
+    pl.semaphore_wait(barrier, 7)
 
     up_a, down_a = dev(ring(a, 1), b), dev(ring(a, 3), b)
     up_b, down_b = dev(a, ring(b, 1)), dev(a, ring(b, 3))
@@ -133,7 +147,6 @@
     go(remote(blk(a, b), blk(a, b), gs.at[1], ga.at[1], down_a))
     spread_b(0, a)
 
-    sibling = t + 1 - 2 * core
     go(remote(wq_hbm, wq.at[:, pl.ds(lane0, HD)], wsend.at[0], wrecv.at[0], sibling))
     go(remote(wkv_hbm, wkv.at[pl.ds(kv_row, 32)], wsend.at[1], wrecv.at[1], sibling))
     go(remote(wo_hbm, wo.at[pl.ds(lane0, HD)], wsend.at[2], wrecv.at[2], sibling))
@@ -174,7 +187,7 @@
         qsend[pl.ds(b_ * 4, 4), :, 2 * HD :] = kv.astype(BF).reshape(4, TOKS, HD)
 
     def post_queries(b_, first):
-        for k in range(first, 4):
+        for k in (2, 1, 3, 0)[: 4 - first]:
             a_ = ring(a, k)
             copy = remote(
                 qsend.at[b_ * 4 + a_], qrecv.at[chip], qs, qr, dev(a_, b_)
@@ -188,7 +201,7 @@
     relay_b(1, am)
     relay_b(2, ap)
 
-    for load in loads[2:4]:
+    for load in loads[2:4] + small[1:]:
         load.wait()
     line = lax.broadcasted_iota(jnp.int32, (2 * N, TOKS), 0)
     expert = line // 2
@@ -214,12 +227,12 @@
         link = jnp.minimum(dot(link.astype(BF), link.astype(BF)), 1.0)
     eye = jnp.where(ri == ci, 1.0, 0.0).astype(BF)
     reach = dot(link.astype(BF), eye, TN)
-    is_tree = kind[0, 0] == 1
+    is_tree = kind[0] == 1
     causal = jnp.where(ci <= ri, 1.0, 0.0)
     allowed = jnp.where(is_tree, reach, causal)
     allow_ref[...] = allowed
     depth = jnp.sum(allowed, axis=1, keepdims=True) - 1.0
-    total = prefix[0, 0] + accepted[0, 0]
+    total = prefix[0] + accepted[0]
     angle = (total.astype(F32) + depth) * freq_ref[...]
     cos_ref[...] = jnp.cos(angle)
     lane_row = lax.broadcasted_iota(jnp.int32, (TOKS, HD), 1)
@@ -235,13 +248,14 @@
     for j, a_ in enumerate((a, am, ap, af)):
         await_bytes(half(a_, bf, 0), gbh.at[j, 0])
         await_bytes(half(a_, bf, 1), gbh.at[j, 1])
+    pl.semaphore_signal(meet, inc=1, device_id={"tensor": sibling}, device_id_type=MESH)
     project(bf)
     post_queries(bf, 0)
 
     row = lax.broadcasted_iota(jnp.int32, (1, CACHE), 1)
-    seen = (row < prefix[0, 0]) & ((row < SINK) | (row >= total - WIN))
+    seen = (row < prefix[0]) & ((row < SINK) | (row >= total - WIN))
     for m in range(8):
-        seen = seen | ((row == prefix[0, 0] + path[0, m]) & (accepted[0, 0] > m))
+        seen = seen | ((row == prefix[0] + path[0, m]) & (accepted[0] > m))
     for load in loads[5:7]:
         load.wait()
     await_bytes(qrecv.at[pl.ds(0, 15)], qr)
@@ -351,13 +365,14 @@
     dsend[...] = fs[...].astype(BF).reshape(N, 32, HD)
 
     def post(src, dst, ssem, rsem):
-        def one(k, carry):
-            to = lax.rem(t + k, N)
-            remote(src.at[to], dst.at[t], ssem, rsem, to).start()
-            return carry
-
-        lax.fori_loop(1, N, one, 0)
-
+        for da, db in FAR_FIRST:
+            for other in range(2):
+                if (da, db, other) == (0, 0, 0):
+                    continue
+                to = dev(ring(a, da), ring(b, db)) + other * (1 - 2 * core)
+                remote(src.at[to], dst.at[t], ssem, rsem, to).start()
+
+    pl.semaphore_wait(meet, 1)
     post(dsend, drecv, ds, dr)
     drecv[t] = dsend[t]
     for load in loads[7:]:
@@ -403,16 +418,20 @@
     freq = np.exp(-(2.0 * half / HD) * math.log(ROPE_BASE)).astype(np.float32)
     freq = jnp.asarray(np.concatenate([freq, freq])[None, :])
     vmem = pl.BlockSpec(memory_space=pltpu.VMEM)
-    smem = pl.BlockSpec(memory_space=pltpu.SMEM)
+    sm = pltpu.SMEM
     hbm = pl.BlockSpec(memory_space=pltpu.HBM)
     dma = pltpu.SemaphoreType.DMA
     vm = pltpu.VMEM
     return pl.pallas_call(
         layer_kernel,
         out_shape=jax.ShapeDtypeStruct((TOKS, D), BF),
-        in_specs=[vmem] * 6 + [smem] * 4 + [hbm] * 11,
+        in_specs=[hbm] * 21,
         out_specs=vmem,
         scratch_shapes=[
+            vm((1, HD), F32),
+            vm((D,), F32), vm((HD,), F32), vm((HD,), F32), vm((D,), F32),
+            vm((1, TOKS), jnp.int32),
+            sm((1,), jnp.int32), sm((1,), jnp.int32), sm((1, 8), jnp.int32), sm((1,), jnp.int32),
             vm((TOKS, D), BF),
             vm((D, 2 * HD), BF),
             vm((HD, D), BF),
@@ -451,6 +470,8 @@
             vm((TOKS, HD), F32),
             vm((TOKS, TOKS), F32),
             dma((11,)),
+            dma((10,)),
+            pltpu.SemaphoreType.REGULAR,
             dma((3,)), dma((3,)),
             dma((10,)),
             dma((2,)), dma((2,)),
@@ -468,7 +489,7 @@
         name="layer",
     )(
         freq, attn_gain, query_gain, key_gain, ffn_gain, parents,
-        prefix_lens[None], accepted[None], accept_path, slot_kinds[None],
+        prefix_lens, accepted, accept_path, slot_kinds,
         residual_in, w_query, w_keyval, w_out, w_gate, w_up, w_down,
         key_cache, value_cache, expert_ids.T, gate_probs.T,
     )

time: 81.6 us -> 75.5 us (0.925)
  Pallas kernels: 77.9 us -> 71.9 us
    pallas_call x1, Pallas kernels: 77.9 us -> 71.9 us  [body(): pl.pallas_call(layer_kernel, out_shape=jax.ShapeDtypeStruct((TOKS, D), BF...]
where the time goes in v2:
time: 75.5 us; the launch traced here: 75.4 us
  Pallas kernels  71.9 us (95%)
  between operations  1.95 us (3%)
  local copies, waits for them, and re-layouts  1.57 us (2%)
    pallas_call x1, Pallas kernels, body(): pl.pallas_call(layer_kernel, out_shape=jax.ShapeDtypeStruct((TOKS, D), BF...  71.9 us
    unnamed x1, local copies, waits for them, and re-layouts  1.57 us

profile of v2, /device:TPU:1, one launch (start us, length us, event | category | flops | bytes accessed | tf_op | source)
XLA Modules:
  0.0 75.4 jit_solution(3295608182561291880)
XLA Ops:
  1.9 71.9 %layer.1 = bf16[32,2048]{1,0:T(8,128)(2,1)} custom-call(f32[1,128]{1,0:T(1,128)} %constant.2.clone.freq_hbm, f32[2048]{0:T(1024)} %again_hbm.1, f32[128]{0:T(128)} %qgain_hbm.1, f32[128]{0:T(128)} %kgain_hbm.1, f32[2048]{0:T(1024)} %fgain_hbm.1, s32[1,32]{1,0:T(1,128)} %par_hbm.1, s32[1]{0:T(128)S(6)} %copy.23.prefix_hbm, s32[1]{0:T(128)S(6)} %copy.24.acc_hbm, ...), custom_call_target="tpu_custom_call" | custom-call | tf_op jit(solution)/shard_map/layer/pallas_call | solution.py:425
  73.9 1.6 %copy.26 = bf16[32,2048]{1,0:T(8,128)(2,1)} copy(bf16[32,2048]{1,0:T(8,128)(2,1)} %layer.1) | data formatting | bytes 262144

commit v3 on v2

v3 whole, which is shorter than its diff:
```python
import functools
import math

import jax
import jax.numpy as jnp
import numpy as np
from jax import lax
from jax.experimental import pallas as pl
from jax.experimental.pallas import tpu as pltpu
from jax.sharding import PartitionSpec as P

SINK = 4
WIN = 512
EPSILON = 1e-06
NEG_FILL = -1e30
ROPE_BASE = 1000000.0

N = 32
TOKS = 32
HT = 16
D = 2048
HD = 128
FF = 768
CACHE = 1024
SCALE = HD**-0.5
LOG2E = math.log2(math.e)

BF = jnp.bfloat16
F32 = jnp.float32
MESH = pl.DeviceIdType.MESH
FAR_FIRST = sorted(
    ((i, j) for i in range(4) for j in range(4)),
    key=lambda ij: -(min(ij[0], 4 - ij[0]) + min(ij[1], 4 - ij[1])),
)
NT = (((1,), (1,)), ((), ()))
TN = (((0,), (0,)), ((), ()))


def dot(a, b, dims=(((1,), (0,)), ((), ()))):
    return lax.dot_general(a, b, dims, preferred_element_type=F32)


def layer_kernel(
    freq_hbm, again_hbm, qgain_hbm, kgain_hbm, fgain_hbm, par_hbm, prefix_hbm, acc_hbm, path_hbm, kind_hbm,
    res_hbm, wq_hbm, wkv_hbm, wo_hbm, wg_hbm, wu_hbm, wd_hbm, kc_hbm, vc_hbm, ids_hbm, gates_hbm,
    out_ref,
    freq_ref, attn_gain, query_gain, key_gain, ffn_gain, parents, prefix, accepted, path, kind,
    res, wq, wkv, wo, wg, wu, wd, kc, vc, ids, gates,
    ag, qsend, qrecv, knew, vnew, asend, ain,
    part, s1, r1, s2, r2, u1, v1, u2, v2, rown, hid, nffn,
    fs, xs, dsend, drecv, ysend, yrecv, sel_ref, comb_ref, cos_ref, sin_ref, allow_ref, seen_ref,
    lsem, isem, meet, snd, rcv, qs, qr, asem, ar, ds, dr, ys, yr,
):
    t = lax.axis_index("tensor")
    core = lax.rem(t, 2)
    chip = t // 2
    cx = chip // 4
    cy = lax.rem(chip, 4)
    a = cx * (1 - core) + cy * core
    b = cy * (1 - core) + cx * core
    step_a = 8 - 6 * core
    step_b = 2 + 6 * core

    def dev(a_, b_):
        return a_ * step_a + b_ * step_b + core

    def ring(v, k):
        return lax.rem(v + k, 4)

    def remote(src, dst, ssem, rsem, to):
        return pltpu.make_async_remote_copy(
            src_ref=src, dst_ref=dst, send_sem=ssem, recv_sem=rsem,
            device_id={"tensor": to}, device_id_type=MESH,
        )

    def await_bytes(ref, sem):
        pltpu.make_async_copy(ref, ref, sem).wait()

    sends = []
    slots = {}

    def slot(key):
        return slots.setdefault(key, len(slots))

    def go(key, src, dst, to):
        copy = remote(src, dst, snd.at[len(sends)], rcv.at[slot(key)], to)
        copy.start()
        sends.append(copy)

    def come(key, ref):
        await_bytes(ref, rcv.at[slot(key)])

    load_res = pltpu.make_async_copy(res_hbm, res, lsem.at[0])
    load_res.start()
    small = [
        pltpu.make_async_copy(src, dst, isem.at[i])
        for i, (src, dst) in enumerate(
            (
                (again_hbm, attn_gain), (freq_hbm, freq_ref), (qgain_hbm, query_gain),
                (kgain_hbm, key_gain), (fgain_hbm, ffn_gain), (par_hbm, parents),
                (prefix_hbm, prefix), (acc_hbm, accepted), (path_hbm, path), (kind_hbm, kind),
            )
        )
    ]
    small[0].start()

    barrier = pltpu.get_barrier_semaphore()
    sibling = t + 1 - 2 * core
    wkv[...] = jnp.zeros_like(wkv)
    line = [dev(ring(a, k), b) for k in (1, 2, 3)] + [dev(a, ring(b, k)) for k in (1, 2, 3)]
    for to in line + [sibling]:
        pl.semaphore_signal(barrier, inc=1, device_id={"tensor": to}, device_id_type=MESH)

    lane0 = pl.multiple_of(core * HD, HD)
    kv_row = pl.multiple_of(lax.rem(chip, 2) * 64 + core * 32, 32)
    lane_win = pl.multiple_of((t // 4) * HD, HD)
    loads = [
        pltpu.make_async_copy(wq_hbm, wq.at[:, pl.ds(lane0, HD)], lsem.at[1]),
        pltpu.make_async_copy(wkv_hbm, wkv.at[pl.ds(kv_row, 32)], lsem.at[2]),
        pltpu.make_async_copy(ids_hbm.at[:, pl.ds(lane_win, HD)], ids, lsem.at[3]),
        pltpu.make_async_copy(gates_hbm.at[:, pl.ds(lane_win, HD)], gates, lsem.at[4]),
        pltpu.make_async_copy(wo_hbm, wo.at[pl.ds(lane0, HD)], lsem.at[5]),
        pltpu.make_async_copy(kc_hbm.at[0], kc, lsem.at[6]),
        pltpu.make_async_copy(vc_hbm.at[0], vc, lsem.at[7]),
        pltpu.make_async_copy(wg_hbm.at[0], wg, lsem.at[8]),
        pltpu.make_async_copy(wu_hbm.at[0], wu, lsem.at[9]),
        pltpu.make_async_copy(wd_hbm.at[0], wd, lsem.at[10]),
    ]
    for load in small[1:] + loads[2:4] + loads[:2] + loads[4:]:
        load.start()

    load_res.wait()
    small[0].wait()
    own = b * 4 + a
    xv = res[...].astype(F32)
    inv = lax.rsqrt(jnp.mean(xv * xv, axis=-1, keepdims=True) + EPSILON)
    normed = (xv * inv * attn_gain[...][None, :]).astype(BF)
    for h in range(2):
        ag[h, own] = normed[HT * h : HT * (h + 1)]

    for load in loads[2:4] + small[1:]:
        load.wait()
    line_no = lax.broadcasted_iota(jnp.int32, (2 * N, TOKS), 0)
    expert = line_no // 2
    named = jnp.zeros((2 * N, TOKS), F32)
    weight = jnp.zeros((2 * N, TOKS), F32)
    turn_lanes = lax.rem(HD - lax.rem(t, 4) * TOKS, HD)
    idv = pltpu.roll(ids[...], turn_lanes, 1)[:, 0:TOKS]
    gv = pltpu.roll(gates[...], turn_lanes, 1)[:, 0:TOKS]
    for k in range(8):
        hit = jnp.broadcast_to(idv[k : k + 1], (2 * N, TOKS)) == expert
        named = jnp.where(hit, 1.0, named)
        weight = weight + jnp.where(hit, jnp.broadcast_to(gv[k : k + 1], (2 * N, TOKS)), 0.0)
    ri = lax.broadcasted_iota(jnp.int32, (TOKS, TOKS), 0)
    ci = lax.broadcasted_iota(jnp.int32, (TOKS, TOKS), 1)
    before = dot(named.astype(BF), jnp.where(ri < ci, 1.0, 0.0).astype(BF))
    turn = lax.rem(line_no, 2).astype(F32)
    taken = (named > 0.5) & (jnp.abs(before - turn) < 0.5)
    sel_ref[...] = jnp.where(taken, 1.0, 0.0).astype(BF)
    comb_ref[...] = jnp.where(taken, weight, 0.0)

    link = jnp.where((ri == jnp.broadcast_to(parents[...], (TOKS, TOKS))) | (ri == ci), 1.0, 0.0)
    for unused in range(5):
        link = jnp.minimum(dot(link.astype(BF), link.astype(BF)), 1.0)
    eye = jnp.where(ri == ci, 1.0, 0.0).astype(BF)
    reach = dot(link.astype(BF), eye, TN)
    is_tree = kind[0] == 1
    causal = jnp.where(ci <= ri, 1.0, 0.0)
    allowed = jnp.where(is_tree, reach, causal)
    allow_ref[...] = allowed
    depth = jnp.sum(allowed, axis=1, keepdims=True) - 1.0
    total = prefix[0] + accepted[0]
    angle = (total.astype(F32) + depth) * freq_ref[...]
    cos_ref[...] = jnp.cos(angle)
    lane_row = lax.broadcasted_iota(jnp.int32, (TOKS, HD), 1)
    sine = jnp.sin(angle)
    sin_ref[...] = jnp.where(lane_row < HD // 2, -sine, sine)
    row = lax.broadcasted_iota(jnp.int32, (1, CACHE), 1)
    seen = (row < prefix[0]) & ((row < SINK) | (row >= total - WIN))
    for m in range(8):
        seen = seen | ((row == prefix[0] + path[0, m]) & (accepted[0] > m))
    seen_ref[...] = jnp.where(seen, 1.0, 0.0)

    pl.semaphore_wait(barrier, 7)

    up_a, down_a = dev(ring(a, 1), b), dev(ring(a, 3), b)
    up_b, down_b = dev(a, ring(b, 1)), dev(a, ring(b, 3))
    am, ap, af = ring(a, 3), ring(a, 1), ring(a, 2)
    bm, bp, bf = ring(b, 3), ring(b, 1), ring(b, 2)
    lo, hi = pl.ds(0, D // 2), pl.ds(D // 2, D // 2)

    def blk(h, a_, b_):
        return ag.at[h, b_ * 4 + a_]

    def side(h, a_, b_, cols):
        return ag.at[h, b_ * 4 + a_, :, cols]

    def start_a(h):
        go(("a", h, 0), blk(h, a, b), blk(h, a, b), up_a)
        go(("a", h, 1), blk(h, a, b), blk(h, a, b), down_a)

    def spread_b(h, j, a_):
        go(("b", h, j, 0), blk(h, a_, b), blk(h, a_, b), up_b)
        go(("b", h, j, 1), blk(h, a_, b), blk(h, a_, b), down_b)

    def relay_a(h):
        come(("a", h, 0), blk(h, am, b))
        go(("ah", h, 0), side(h, am, b, lo), side(h, am, b, lo), up_a)
        spread_b(h, 1, am)
        come(("a", h, 1), blk(h, ap, b))
        go(("ah", h, 1), side(h, ap, b, hi), side(h, ap, b, hi), down_a)
        spread_b(h, 2, ap)

    def far_a(h):
        come(("ah", h, 0), side(h, af, b, lo))
        come(("ah", h, 1), side(h, af, b, hi))
        spread_b(h, 3, af)

    def relay_b(h, j, a_):
        come(("b", h, j, 0), blk(h, a_, bm))
        go(("bh", h, j, 0), side(h, a_, bm, lo), side(h, a_, bm, lo), up_b)
        come(("b", h, j, 1), blk(h, a_, bp))
        go(("bh", h, j, 1), side(h, a_, bp, hi), side(h, a_, bp, hi), down_b)

    def far_b(h):
        for j, a_ in enumerate((a, am, ap, af)):
            come(("bh", h, j, 0), side(h, a_, bf, lo))
            come(("bh", h, j, 1), side(h, a_, bf, hi))

    def project(h, groups):
        rows = jnp.concatenate(
            [ag[h, pl.ds(b_ * 4, 4)].reshape(4 * HT, D) for b_ in groups], axis=0
        )
        q = dot(rows, wq[...]).astype(BF)
        kv = dot(rows, wkv[...], NT).astype(BF)
        for i, b_ in enumerate(groups):
            r = slice(4 * HT * i, 4 * HT * (i + 1))
            qsend[h, pl.ds(b_ * 4, 4), :, 0 : 2 * HD] = q[r].reshape(4, HT, 2 * HD)
            qsend[h, pl.ds(b_ * 4, 4), :, 2 * HD :] = kv[r].reshape(4, HT, HD)

    def post_queries(h, b_, steps=(2, 1, 3, 0)):
        for k in steps:
            a_ = ring(a, k)
            remote(
                qsend.at[h, b_ * 4 + a_], qrecv.at[h, chip], qs.at[h], qr.at[h], dev(a_, b_)
            ).start()

    def project_own(h):
        project(h, (b,))
        qrecv[h, chip] = qsend[h, own]
        post_queries(h, b, (2, 1, 3))

    def project_near(h):
        project(h, (bm, bp))
        post_queries(h, bm)
        post_queries(h, bp)

    def project_far(h):
        project(h, (bf,))
        post_queries(h, bf)

    start_a(0)
    spread_b(0, 0, a)
    start_a(1)
    spread_b(1, 0, a)
    go("wq", wq_hbm, wq.at[:, pl.ds(lane0, HD)], sibling)
    go("wkv", wkv_hbm, wkv.at[pl.ds(kv_row, 32)], sibling)
    go("wo", wo_hbm, wo.at[pl.ds(lane0, HD)], sibling)
    other_lane = pl.multiple_of(HD - core * HD, HD)
    other_row = pl.multiple_of(lax.rem(chip, 2) * 64 + 32 - core * 32, 32)

    relay_a(0)
    relay_b(0, 0, a)
    relay_a(1)
    far_a(0)
    relay_b(1, 0, a)
    for load in loads[:2]:
        load.wait()
    come("wq", wq.at[:, pl.ds(other_lane, HD)])
    come("wkv", wkv.at[pl.ds(other_row, 32)])
    project_own(0)
    relay_b(0, 1, am)
    far_a(1)
    relay_b(0, 2, ap)
    relay_b(0, 3, af)
    project_near(0)
    relay_b(1, 1, am)
    far_b(0)
    project_far(0)
    relay_b(1, 2, ap)
    relay_b(1, 3, af)
    project_own(1)
    project_near(1)
    far_b(1)
    pl.semaphore_signal(meet, inc=1, device_id={"tensor": sibling}, device_id_type=MESH)
    project_far(1)

    for load in loads[5:7]:
        load.wait()

    def attend(h):
        await_bytes(qrecv.at[h, pl.ds(0, 15)], qr.at[h])
        mine = slice(HT * h, HT * (h + 1))
        count = HT * (h + 1)
        cosv, sinv = cos_ref[mine], sin_ref[mine]

        def rope(v, gain):
            v = v * lax.rsqrt(jnp.mean(v * v, axis=-1, keepdims=True) + EPSILON) * gain
            return (v * cosv + pltpu.roll(v, HD // 2, 1) * sinv).astype(BF)

        def heads(g, carry):
            qgain = query_gain[...][None, :]
            qg = jnp.concatenate(
                [
                    rope(qrecv[h, 4 * g + i, :, HD * j : HD * (j + 1)].astype(F32), qgain)
                    for i in range(4)
                    for j in range(2)
                ],
                axis=0,
            )
            kraw = qrecv[h, 2 * g, :, 2 * HD :].astype(F32) + qrecv[h, 2 * g + 1, :, 2 * HD :].astype(F32)
            knew[g, mine] = rope(kraw, key_gain[...][None, :])
            vnew[g, mine] = qrecv[h, 8 + 2 * g, :, 2 * HD :] + qrecv[h, 9 + 2 * g, :, 2 * HD :]
            cols = pl.ds(pl.multiple_of(g * HD, HD), HD)
            s_old = dot(qg, kc[:, cols], NT)
            s_new = dot(qg, knew[g, 0:count], NT)
            s_old = jnp.where(jnp.broadcast_to(seen_ref[...], s_old.shape) > 0.5, s_old, NEG_FILL)
            allow = jnp.concatenate([allow_ref[mine, 0:count]] * 8, axis=0)
            s_new = jnp.where(allow > 0.5, s_new, NEG_FILL)
            top = jnp.maximum(
                jnp.max(s_old, axis=-1, keepdims=True), jnp.max(s_new, axis=-1, keepdims=True)
            )
            e_old = jnp.exp2((s_old - top) * (SCALE * LOG2E))
            e_new = jnp.exp2((s_new - top) * (SCALE * LOG2E))
            denom = jnp.sum(e_old, axis=-1, keepdims=True) + jnp.sum(e_new, axis=-1, keepdims=True)
            o = dot(e_old.astype(BF), vc[:, cols]) + dot(e_new.astype(BF), vnew[g, 0:count])
            o = (o / denom).astype(BF)
            for i in range(4):
                to = 4 * g + i
                for j in range(2):
                    r0 = (2 * i + j) * HT
                    asend[h, to, :, HD * j : HD * (j + 1)] = o[r0 : r0 + HT]

                @pl.when(to != chip)
                def _():
                    remote(
                        asend.at[h, to], ain.at[h, own], asem.at[h], ar.at[h, b], 2 * to + core
                    ).start()

            return carry

        lax.fori_loop(0, 4, heads, 0)
        ain[h, own] = asend[h, chip]

    order = (bf, bp, bm, b)
    left, right = slice(0, D // 2), slice(D // 2, D)

    def piece(h, k, a_):
        return part[h, k, pl.ds(pl.multiple_of(a_ * HT, HT), HT), :]

    def sum_first(h):
        for k, b_ in enumerate(order):
            await_bytes(ain.at[h, pl.ds(b_ * 4, 3 if k == 3 else 4)], ar.at[h, b_])
            part[h, k] = dot(ain[h, pl.ds(b_ * 4, 4)].reshape(4 * HT, 2 * HD), wo[...])
            far = piece(h, k, af).astype(BF)
            s1[h, k, 0] = far[:, left]
            go(("s", h, k, 0), s1.at[h, k, 0], r1.at[h, k, 0], up_a)
            s1[h, k, 1] = far[:, right]
            go(("s", h, k, 1), s1.at[h, k, 1], r1.at[h, k, 1], down_a)

    def sum_second(h):
        for k in range(4):
            come(("s", h, k, 0), r1.at[h, k, 0])
            to_up = piece(h, k, ap)
            s2[h, k, 0, :, left] = (to_up[:, left] + r1[h, k, 0].astype(F32)).astype(BF)
            s2[h, k, 0, :, right] = to_up[:, right].astype(BF)
            go(("t", h, k, 0), s2.at[h, k, 0], r2.at[h, k, 0], up_a)
            come(("s", h, k, 1), r1.at[h, k, 1])
            to_down = piece(h, k, am)
            s2[h, k, 1, :, left] = to_down[:, left].astype(BF)
            s2[h, k, 1, :, right] = (to_down[:, right] + r1[h, k, 1].astype(F32)).astype(BF)
            go(("t", h, k, 1), s2.at[h, k, 1], r2.at[h, k, 1], down_a)

    def sum_third(h):
        for k in range(4):
            come(("t", h, k, 0), r2.at[h, k, 0])
            come(("t", h, k, 1), r2.at[h, k, 1])
            rs = piece(h, k, a) + r2[h, k, 0].astype(F32) + r2[h, k, 1].astype(F32)
            if k == 0:
                u1[h, 0] = rs[:, left].astype(BF)
                u1[h, 1] = rs[:, right].astype(BF)
                go(("u", h, 0), u1.at[h, 0], v1.at[h, 0], up_b)
                go(("u", h, 1), u1.at[h, 1], v1.at[h, 1], down_b)
            elif k == 1:
                come(("u", h, 0), v1.at[h, 0])
                u2[h, 0, :, left] = (rs[:, left] + v1[h, 0].astype(F32)).astype(BF)
                u2[h, 0, :, right] = rs[:, right].astype(BF)
                go(("v", h, 0), u2.at[h, 0], v2.at[h, 0], up_b)
            elif k == 2:
                come(("u", h, 1), v1.at[h, 1])
                u2[h, 1, :, left] = rs[:, left].astype(BF)
                u2[h, 1, :, right] = (rs[:, right] + v1[h, 1].astype(F32)).astype(BF)
                go(("v", h, 1), u2.at[h, 1], v2.at[h, 1], down_b)
            else:
                rown[h] = rs

    def finish(h):
        mine = slice(HT * h, HT * (h + 1))
        come(("v", h, 0), v2.at[h, 0])
        come(("v", h, 1), v2.at[h, 1])
        hidden = res[mine].astype(F32) + (
            rown[h] + v2[h, 0].astype(F32) + v2[h, 1].astype(F32)
        )
        hid[mine] = hidden
        scale = lax.rsqrt(jnp.mean(hidden * hidden, axis=-1, keepdims=True) + EPSILON)
        nffn[mine] = (hidden * scale * ffn_gain[...][None, :]).astype(BF)

    attend(0)
    loads[4].wait()
    come("wo", wo.at[pl.ds(other_lane, HD)])
    sum_first(0)
    attend(1)
    sum_second(0)
    sum_first(1)
    sum_third(0)
    sum_second(1)
    finish(0)
    sum_third(1)
    finish(1)

    picked = dot(sel_ref[...], nffn[...])
    for j in range(16):
        fs[pl.ds(j, 64, stride=16), :] = picked[:, HD * j : HD * (j + 1)]
    dsend[...] = fs[...].astype(BF).reshape(N, 32, HD)

    def post(src, dst, ssem, rsem):
        for da, db in FAR_FIRST:
            for other in range(2):
                if (da, db, other) == (0, 0, 0):
                    continue
                to = dev(ring(a, da), ring(b, db)) + other * (1 - 2 * core)
                remote(src.at[to], dst.at[t], ssem, rsem, to).start()

    pl.semaphore_wait(meet, 1)
    post(dsend, drecv, ds, dr)
    drecv[t] = dsend[t]
    for load in loads[7:]:
        load.wait()
    await_bytes(drecv.at[pl.ds(0, N - 1)], dr)
    fs[...] = drecv[...].reshape(1024, HD).astype(F32)
    for j in range(16):
        xs[:, HD * j : HD * (j + 1)] = fs[pl.ds(j, 64, stride=16), :].astype(BF)
    gate = dot(xs[...], wg[...], NT)
    up = dot(xs[...], wu[...], NT)
    inner = (gate / (1.0 + jnp.exp(-gate)) * up).astype(BF)
    y = dot(inner, wd[...])
    for j in range(16):
        fs[pl.ds(j, 64, stride=16), :] = y[:, HD * j : HD * (j + 1)]
    ysend[...] = fs[...].astype(BF).reshape(N, 32, HD)
    post(ysend, yrecv, ys, yr)
    yrecv[t] = ysend[t]
    await_bytes(yrecv.at[pl.ds(0, N - 1)], yr)
    fs[...] = yrecv[...].reshape(1024, HD).astype(F32)
    comb = comb_ref[...]
    comb_hi = comb.astype(BF)
    comb_lo = (comb - comb_hi.astype(F32)).astype(BF)
    for j in range(16):
        yj = fs[pl.ds(j, 64, stride=16), :].astype(BF)
        moe = dot(comb_hi, yj, TN) + dot(comb_lo, yj, TN)
        cols = slice(HD * j, HD * (j + 1))
        out_ref[:, cols] = (hid[:, cols] + moe).astype(BF)

    for copy in sends:
        copy.wait_send()
    for h in range(2):
        await_bytes(qsend.at[h, pl.ds(0, 15)], qs.at[h])
        await_bytes(asend.at[h, pl.ds(0, 15)], asem.at[h])
    await_bytes(dsend.at[pl.ds(0, N - 1)], ds)
    await_bytes(ysend.at[pl.ds(0, N - 1)], ys)


def body(
    residual_in, attn_gain, w_query, w_keyval, query_gain, key_gain, w_out, ffn_gain,
    w_gate, w_up, w_down, key_cache, value_cache, prefix_lens, accepted, accept_path,
    parents, slot_kinds, expert_ids, gate_probs,
):
    half = np.arange(HD // 2, dtype=np.float64)
    freq = np.exp(-(2.0 * half / HD) * math.log(ROPE_BASE)).astype(np.float32)
    freq = jnp.asarray(np.concatenate([freq, freq])[None, :])
    vmem = pl.BlockSpec(memory_space=pltpu.VMEM)
    sm = pltpu.SMEM
    hbm = pl.BlockSpec(memory_space=pltpu.HBM)
    dma = pltpu.SemaphoreType.DMA
    vm = pltpu.VMEM
    return pl.pallas_call(
        layer_kernel,
        out_shape=jax.ShapeDtypeStruct((TOKS, D), BF),
        in_specs=[hbm] * 21,
        out_specs=vmem,
        scratch_shapes=[
            vm((1, HD), F32),
            vm((D,), F32), vm((HD,), F32), vm((HD,), F32), vm((D,), F32),
            vm((1, TOKS), jnp.int32),
            sm((1,), jnp.int32), sm((1,), jnp.int32), sm((1, 8), jnp.int32), sm((1,), jnp.int32),
            vm((TOKS, D), BF),
            vm((D, 2 * HD), BF),
            vm((HD, D), BF),
            vm((2 * HD, D), BF),
            vm((FF, D), BF),
            vm((FF, D), BF),
            vm((FF, D), BF),
            vm((CACHE, 4 * HD), BF),
            vm((CACHE, 4 * HD), BF),
            vm((8, HD), jnp.int32),
            vm((8, HD), F32),
            vm((2, 16, HT, D), BF),
            vm((2, 16, HT, 3 * HD), BF),
            vm((2, 16, HT, 3 * HD), BF),
            vm((4, TOKS, HD), BF),
            vm((4, TOKS, HD), BF),
            vm((2, 16, HT, 2 * HD), BF),
            vm((2, 16, HT, 2 * HD), BF),
            vm((2, 4, 4 * HT, D), F32),
            vm((2, 4, 2, HT, D // 2), BF),
            vm((2, 4, 2, HT, D // 2), BF),
            vm((2, 4, 2, HT, D), BF),
            vm((2, 4, 2, HT, D), BF),
            vm((2, 2, HT, D // 2), BF),
            vm((2, 2, HT, D // 2), BF),
            vm((2, 2, HT, D), BF),
            vm((2, 2, HT, D), BF),
            vm((2, HT, D), F32),
            vm((TOKS, D), F32),
            vm((TOKS, D), BF),
            vm((1024, HD), F32),
            vm((2 * N, D), BF),
            vm((N, 32, HD), BF),
            vm((N, 32, HD), BF),
            vm((N, 32, HD), BF),
            vm((N, 32, HD), BF),
            vm((2 * N, TOKS), BF),
            vm((2 * N, TOKS), F32),
            vm((TOKS, HD), F32),
            vm((TOKS, HD), F32),
            vm((TOKS, TOKS), F32),
            vm((1, CACHE), F32),
            dma((11,)),
            dma((10,)),
            pltpu.SemaphoreType.REGULAR,
            dma((83,)), dma((83,)),
            dma((2,)), dma((2,)),
            dma((2,)), dma((2, 4)),
            dma(()), dma(()), dma(()), dma(()),
        ],
        compiler_params=pltpu.CompilerParams(
            collective_id=0, has_side_effects=True, vmem_limit_bytes=56 * 1024 * 1024
        ),
        name="layer",
    )(
        freq, attn_gain, query_gain, key_gain, ffn_gain, parents,
        prefix_lens, accepted, accept_path, slot_kinds,
        residual_in, w_query, w_keyval, w_out, w_gate, w_up, w_down,
        key_cache, value_cache, expert_ids.T, gate_probs.T,
    )


def solution(mesh):
    in_specs = (
        P(("group", "tensor"), None),
        P(),
        P(None, "tensor"),
        P("tensor", None),
        P(),
        P(),
        P("tensor", None),
        P(),
        P("tensor", None, None),
        P("tensor", None, None),
        P("tensor", None, None),
        P(("group", "tensor"), None, None),
        P(("group", "tensor"), None, None),
        P(("group", "tensor")),
        P(("group", "tensor")),
        P(("group", "tensor"), None),
        P(("group", "tensor"), None),
        P(("group", "tensor")),
        P("group", None),
        P("group", None),
    )
    out_specs = P(("group", "tensor"), None)
    return jax.shard_map(body, mesh=mesh, in_specs=in_specs, out_specs=out_specs, check_vma=False)
```

time: 75.5 us -> 79.7 us (1.056)
  Pallas kernels: 71.9 us -> 76.1 us
    pallas_call x1, Pallas kernels: 71.9 us -> 76.1 us  [body(): pl.pallas_call(layer_kernel, out_shape=jax.ShapeDtypeStruct((TOKS, D), BF...]
where the time goes in v3:
time: 79.7 us; the launch traced here: 79.6 us
  Pallas kernels  76.1 us (95%)
  between operations  1.95 us (2%)
  local copies, waits for them, and re-layouts  1.57 us (2%)
    pallas_call x1, Pallas kernels, body(): pl.pallas_call(layer_kernel, out_shape=jax.ShapeDtypeStruct((TOKS, D), BF...  76.1 us

profile of v3, /device:TPU:1, one launch (start us, length us, event | category | flops | bytes accessed | tf_op | source)
XLA Modules:
  0.0 79.6 jit_solution(3196446766274396121)
XLA Ops:
  1.9 76.1 %layer.1 = bf16[32,2048]{1,0:T(8,128)(2,1)} custom-call(f32[1,128]{1,0:T(1,128)} %constant.2.clone.freq_hbm, f32[2048]{0:T(1024)} %again_hbm.1, f32[128]{0:T(128)} %qgain_hbm.1, f32[128]{0:T(128)} %kgain_hbm.1, f32[2048]{0:T(1024)} %fgain_hbm.1, s32[1,32]{1,0:T(1,128)} %par_hbm.1, s32[1]{0:T(128)S(6)} %copy.23.prefix_hbm, s32[1]{0:T(128)S(6)} %copy.24.acc_hbm, ...), custom_call_target="tpu_custom_call" | custom-call | tf_op jit(solution)/shard_map/layer/pallas_call | solution.py:495
  78.0 1.6 %copy.26 = bf16[32,2048]{1,0:T(8,128)(2,1)} copy(bf16[32,2048]{1,0:T(8,128)(2,1)} %layer.1) | data formatting | bytes 262144

commit v4 on v2

--- a/solution.py
+++ b/solution.py
@@ -46,10 +46,10 @@
     freq_ref, attn_gain, query_gain, key_gain, ffn_gain, parents, prefix, accepted, path, kind,
     res, wq, wkv, wo, wg, wu, wd, kc, vc, ids, gates,
     ag, qsend, qrecv, asend, ain,
-    part, s1, r1, s2, r2, u1, v1, u2, v2, rsum,
-    fs, xs, dsend, drecv, ysend, yrecv, sel_ref, comb_ref, cos_ref, sin_ref, allow_ref,
-    lsem, isem, meet, wsend, wrecv, gs, ga, gh, gb, gbh, hs, qs, qr, asem, ar,
-    t1s, t1r, t2s, t2r, p1s, p1r, p2s, p2r, ds, dr, ys, yr,
+    pup, pdown, pown, s1, r1, s2, r2, v1, v2, hid,
+    fs, xs, dsend, drecv, ysend, yrecv, sel_ref, comb_ref, link_ref,
+    qcos, qsin, kcos, ksin, allow_ref, seen_ref,
+    lsem, isem, meet, snd, rcv, qs, qr, asem, ar, ds, dr, ys, yr,
 ):
     t = lax.axis_index("tensor")
     core = lax.rem(t, 2)
@@ -75,6 +75,20 @@
 
     def await_bytes(ref, sem):
         pltpu.make_async_copy(ref, ref, sem).wait()
+
+    sends = []
+    slots = {}
+
+    def slot(key):
+        return slots.setdefault(key, len(slots))
+
+    def go(key, src, dst, to):
+        copy = remote(src, dst, snd.at[len(sends)], rcv.at[slot(key)], to)
+        copy.start()
+        sends.append(copy)
+
+    def come(key, ref):
+        await_bytes(ref, rcv.at[slot(key)])
 
     load_res = pltpu.make_async_copy(res_hbm, res, lsem.at[0])
     load_res.start()
@@ -105,7 +119,7 @@
         pltpu.make_async_copy(wu_hbm.at[0], wu, lsem.at[9]),
         pltpu.make_async_copy(wd_hbm.at[0], wd, lsem.at[10]),
     ]
-    for load in loads[:2] + small[1:] + loads[2:]:
+    for load in loads[2:4] + small[1:] + loads[:2] + loads[4:]:
         load.start()
 
     barrier = pltpu.get_barrier_semaphore()
@@ -121,85 +135,6 @@
     xv = res[...].astype(F32)
     inv = lax.rsqrt(jnp.mean(xv * xv, axis=-1, keepdims=True) + EPSILON)
     ag[own] = (xv * inv * attn_gain[...][None, :]).astype(BF)
-
-    pl.semaphore_wait(barrier, 7)
-
-    up_a, down_a = dev(ring(a, 1), b), dev(ring(a, 3), b)
-    up_b, down_b = dev(a, ring(b, 1)), dev(a, ring(b, 3))
-
-    def blk(a_, b_):
-        return ag.at[b_ * 4 + a_]
-
-    def half(a_, b_, h):
-        return ag.at[b_ * 4 + a_, pl.ds(16 * h, 16)]
-
-    sends = []
-
-    def go(copy):
-        copy.start()
-        sends.append(copy)
-
-    def spread_b(j, a_):
-        go(remote(blk(a_, b), blk(a_, b), gs.at[2 + 2 * j], gb.at[j, 0], up_b))
-        go(remote(blk(a_, b), blk(a_, b), gs.at[3 + 2 * j], gb.at[j, 1], down_b))
-
-    go(remote(blk(a, b), blk(a, b), gs.at[0], ga.at[0], up_a))
-    go(remote(blk(a, b), blk(a, b), gs.at[1], ga.at[1], down_a))
-    spread_b(0, a)
-
-    go(remote(wq_hbm, wq.at[:, pl.ds(lane0, HD)], wsend.at[0], wrecv.at[0], sibling))
-    go(remote(wkv_hbm, wkv.at[pl.ds(kv_row, 32)], wsend.at[1], wrecv.at[1], sibling))
-    go(remote(wo_hbm, wo.at[pl.ds(lane0, HD)], wsend.at[2], wrecv.at[2], sibling))
-
-    am, ap, af = ring(a, 3), ring(a, 1), ring(a, 2)
-    bm, bp, bf = ring(b, 3), ring(b, 1), ring(b, 2)
-
-    await_bytes(blk(am, b), ga.at[0])
-    go(remote(half(am, b, 0), half(am, b, 0), hs.at[0], gh.at[0], up_a))
-    spread_b(1, am)
-    await_bytes(blk(ap, b), ga.at[1])
-    go(remote(half(ap, b, 1), half(ap, b, 1), hs.at[1], gh.at[1], down_a))
-    spread_b(2, ap)
-
-    def relay_b(j, a_):
-        await_bytes(blk(a_, bm), gb.at[j, 0])
-        go(remote(half(a_, bm, 0), half(a_, bm, 0), hs.at[2 + 2 * j], gbh.at[j, 0], up_b))
-        await_bytes(blk(a_, bp), gb.at[j, 1])
-        go(remote(half(a_, bp, 1), half(a_, bp, 1), hs.at[3 + 2 * j], gbh.at[j, 1], down_b))
-
-    relay_b(0, a)
-    await_bytes(half(af, b, 0), gh.at[0])
-    await_bytes(half(af, b, 1), gh.at[1])
-    spread_b(3, af)
-
-    for load in loads[:2]:
-        load.wait()
-    other_lane = pl.multiple_of(HD - core * HD, HD)
-    other_row = pl.multiple_of(lax.rem(chip, 2) * 64 + 32 - core * 32, 32)
-    await_bytes(wq.at[:, pl.ds(other_lane, HD)], wrecv.at[0])
-    await_bytes(wkv.at[pl.ds(other_row, 32)], wrecv.at[1])
-
-    def project(b_):
-        rows = ag[pl.ds(b_ * 4, 4)].reshape(4 * TOKS, D)
-        q = dot(rows, wq[...])
-        kv = dot(rows, wkv[...], NT)
-        qsend[pl.ds(b_ * 4, 4), :, 0 : 2 * HD] = q.astype(BF).reshape(4, TOKS, 2 * HD)
-        qsend[pl.ds(b_ * 4, 4), :, 2 * HD :] = kv.astype(BF).reshape(4, TOKS, HD)
-
-    def post_queries(b_, first):
-        for k in (2, 1, 3, 0)[: 4 - first]:
-            a_ = ring(a, k)
-            copy = remote(
-                qsend.at[b_ * 4 + a_], qrecv.at[chip], qs, qr, dev(a_, b_)
-            )
-            copy.start()
-
-    project(b)
-    qrecv[chip] = qsend[own]
-    post_queries(b, 1)
-
-    relay_b(1, am)
-    relay_b(2, ap)
 
     for load in loads[2:4] + small[1:]:
         load.wait()
@@ -225,64 +160,143 @@
     link = jnp.where((ri == jnp.broadcast_to(parents[...], (TOKS, TOKS))) | (ri == ci), 1.0, 0.0)
     for unused in range(5):
         link = jnp.minimum(dot(link.astype(BF), link.astype(BF)), 1.0)
+    link_ref[...] = link.astype(BF)
+
+    pl.semaphore_wait(barrier, 7)
+
+    up_a, down_a = dev(ring(a, 1), b), dev(ring(a, 3), b)
+    up_b, down_b = dev(a, ring(b, 1)), dev(a, ring(b, 3))
+
+    def blk(a_, b_):
+        return ag.at[b_ * 4 + a_]
+
+    def half(a_, b_, h):
+        return ag.at[b_ * 4 + a_, pl.ds(16 * h, 16)]
+
+    def spread_b(j, a_):
+        go(("b", j, 0), blk(a_, b), blk(a_, b), up_b)
+        go(("b", j, 1), blk(a_, b), blk(a_, b), down_b)
+
+    am, ap, af = ring(a, 3), ring(a, 1), ring(a, 2)
+    bm, bp, bf = ring(b, 3), ring(b, 1), ring(b, 2)
+    go(("a", 0), blk(a, b), blk(a, b), up_a)
+    go(("a", 1), blk(a, b), blk(a, b), down_a)
+    spread_b(0, a)
+    go(("a", 2), blk(a, b), blk(a, b), dev(af, b))
+    go("wq", wq_hbm, wq.at[:, pl.ds(lane0, HD)], sibling)
+    go("wkv", wkv_hbm, wkv.at[pl.ds(kv_row, 32)], sibling)
+    go("wo", wo_hbm, wo.at[pl.ds(lane0, HD)], sibling)
+
     eye = jnp.where(ri == ci, 1.0, 0.0).astype(BF)
-    reach = dot(link.astype(BF), eye, TN)
-    is_tree = kind[0] == 1
-    causal = jnp.where(ci <= ri, 1.0, 0.0)
-    allowed = jnp.where(is_tree, reach, causal)
-    allow_ref[...] = allowed
+    reach = dot(link_ref[...], eye, TN)
+    allowed = jnp.where(kind[0] == 1, reach, jnp.where(ci <= ri, 1.0, 0.0))
+    allow_ref[...] = jnp.where(allowed > 0.5, 0.0, NEG_FILL)
     depth = jnp.sum(allowed, axis=1, keepdims=True) - 1.0
     total = prefix[0] + accepted[0]
     angle = (total.astype(F32) + depth) * freq_ref[...]
-    cos_ref[...] = jnp.cos(angle)
-    lane_row = lax.broadcasted_iota(jnp.int32, (TOKS, HD), 1)
+    cosine = jnp.cos(angle)
+    lane = lax.broadcasted_iota(jnp.int32, (TOKS, HD), 1)
     sine = jnp.sin(angle)
-    sin_ref[...] = jnp.where(lane_row < HD // 2, -sine, sine)
-
-    relay_b(3, af)
-    project(bm)
-    post_queries(bm, 0)
-    project(bp)
-    post_queries(bp, 0)
-
-    for j, a_ in enumerate((a, am, ap, af)):
-        await_bytes(half(a_, bf, 0), gbh.at[j, 0])
-        await_bytes(half(a_, bf, 1), gbh.at[j, 1])
-    pl.semaphore_signal(meet, inc=1, device_id={"tensor": sibling}, device_id_type=MESH)
-    project(bf)
-    post_queries(bf, 0)
-
+    sine = jnp.where(lane < HD // 2, -sine, sine)
+    for gain_ref, cos_ref, sin_ref in ((query_gain, qcos, qsin), (key_gain, kcos, ksin)):
+        gain = jnp.broadcast_to(gain_ref[...][None, :], (TOKS, HD))
+        cos_ref[...] = cosine * gain
+        sin_ref[...] = sine * pltpu.roll(gain, HD // 2, 1)
     row = lax.broadcasted_iota(jnp.int32, (1, CACHE), 1)
     seen = (row < prefix[0]) & ((row < SINK) | (row >= total - WIN))
     for m in range(8):
         seen = seen | ((row == prefix[0] + path[0, m]) & (accepted[0] > m))
+    seen_ref[...] = jnp.where(seen, 0.0, NEG_FILL)
+
+    come(("a", 0), blk(am, b))
+    spread_b(1, am)
+    come(("a", 1), blk(ap, b))
+    spread_b(2, ap)
+
+    def relay_b(j, a_):
+        come(("b", j, 0), blk(a_, bm))
+        go(("bh", j, 0), half(a_, bm, 0), half(a_, bm, 0), up_b)
+        come(("b", j, 1), blk(a_, bp))
+        go(("bh", j, 1), half(a_, bp, 1), half(a_, bp, 1), down_b)
+
+    relay_b(0, a)
+    come(("a", 2), blk(af, b))
+    spread_b(3, af)
+    go(("b", 3, 2), blk(af, b), blk(af, b), dev(a, bf))
+
+    for load in loads[:2]:
+        load.wait()
+    other_lane = pl.multiple_of(HD - core * HD, HD)
+    other_row = pl.multiple_of(lax.rem(chip, 2) * 64 + 32 - core * 32, 32)
+    come("wq", wq.at[:, pl.ds(other_lane, HD)])
+    come("wkv", wkv.at[pl.ds(other_row, 32)])
+
+    def project(b_):
+        rows = ag[pl.ds(b_ * 4, 4)].reshape(4 * TOKS, D)
+        q = dot(rows, wq[...])
+        kv = dot(rows, wkv[...], NT)
+        qsend[pl.ds(b_ * 4, 4), :, 0 : 2 * HD] = q.astype(BF).reshape(4, TOKS, 2 * HD)
+        qsend[pl.ds(b_ * 4, 4), :, 2 * HD :] = kv.astype(BF).reshape(4, TOKS, HD)
+
+    def post_queries(b_, first):
+        for k in (2, 1, 3, 0)[: 4 - first]:
+            a_ = ring(a, k)
+            copy = remote(
+                qsend.at[b_ * 4 + a_], qrecv.at[chip], qs, qr, dev(a_, b_)
+            )
+            copy.start()
+
+    project(b)
+    qrecv[chip] = qsend[own]
+    post_queries(b, 1)
+
+    relay_b(1, am)
+    relay_b(2, ap)
+    come(("b", 3, 0), blk(af, bm))
+    project(bm)
+    post_queries(bm, 0)
+    come(("b", 3, 1), blk(af, bp))
+    project(bp)
+    post_queries(bp, 0)
+    for j, a_ in enumerate((a, am, ap)):
+        come(("bh", j, 0), half(a_, bf, 0))
+        come(("bh", j, 1), half(a_, bf, 1))
+    come(("b", 3, 2), blk(af, bf))
+    pl.semaphore_signal(meet, inc=1, device_id={"tensor": sibling}, device_id_type=MESH)
+    project(bf)
+    post_queries(bf, 0)
+
     for load in loads[5:7]:
         load.wait()
     await_bytes(qrecv.at[pl.ds(0, 15)], qr)
 
-    def rope(v, gain):
-        v = v * lax.rsqrt(jnp.mean(v * v, axis=-1, keepdims=True) + EPSILON) * gain
-        return (v * cos_ref[...] + pltpu.roll(v, HD // 2, 1) * sin_ref[...]).astype(BF)
+    ones = jnp.ones((HD, HD), BF)
+
+    def rope(v, cosv, sinv):
+        count = v.shape[0]
+        v = v.reshape(count * TOKS, HD)
+        square = v * v
+        upper = square.astype(BF)
+        lower = (square - upper.astype(F32)).astype(BF)
+        mean = (dot(upper, ones) + dot(lower, ones)) * (1.0 / HD)
+        turned = (
+            v.reshape(count, TOKS, HD) * cosv[...][None]
+            + pltpu.roll(v, HD // 2, 1).reshape(count, TOKS, HD) * sinv[...][None]
+        )
+        return (turned.reshape(count * TOKS, HD) * lax.rsqrt(mean + EPSILON)).astype(BF)
 
     def heads(g, carry):
-        qgain = query_gain[...][None, :]
-        qg = jnp.concatenate(
-            [
-                rope(qrecv[4 * g + i, :, HD * j : HD * (j + 1)].astype(F32), qgain)
-                for i in range(4)
-                for j in range(2)
-            ],
-            axis=0,
-        )
+        qraw = [
+            qrecv[4 * g + i, :, HD * j : HD * (j + 1)] for i in range(4) for j in range(2)
+        ]
+        qg = rope(jnp.stack(qraw, axis=0).astype(F32), qcos, qsin)
         kraw = qrecv[2 * g, :, 2 * HD :].astype(F32) + qrecv[2 * g + 1, :, 2 * HD :].astype(F32)
-        knew = rope(kraw, key_gain[...][None, :])
+        knew = rope(kraw[None], kcos, ksin)
         vnew = qrecv[8 + 2 * g, :, 2 * HD :] + qrecv[9 + 2 * g, :, 2 * HD :]
         cols = pl.ds(pl.multiple_of(g * HD, HD), HD)
-        s_old = dot(qg, kc[:, cols], NT)
+        s_old = dot(qg, kc[:, cols], NT) + seen_ref[...]
         s_new = dot(qg, knew, NT)
-        s_old = jnp.where(jnp.broadcast_to(seen, s_old.shape), s_old, NEG_FILL)
-        allow = jnp.concatenate([allow_ref[...]] * 8, axis=0)
-        s_new = jnp.where(allow > 0.5, s_new, NEG_FILL)
+        s_new = (s_new.reshape(8, TOKS, TOKS) + allow_ref[...][None]).reshape(8 * TOKS, TOKS)
         top = jnp.maximum(
             jnp.max(s_old, axis=-1, keepdims=True), jnp.max(s_new, axis=-1, keepdims=True)
         )
@@ -307,55 +321,45 @@
     ain[own] = asend[chip]
 
     loads[4].wait()
-    await_bytes(wo.at[pl.ds(other_lane, HD)], wrecv.at[2])
+    come("wo", wo.at[pl.ds(other_lane, HD)])
     order = (bf, bp, bm, b)
     for k, b_ in enumerate(order):
         await_bytes(ain.at[pl.ds(b_ * 4, 3 if k == 3 else 4)], ar.at[b_])
-        part[k] = dot(ain[pl.ds(b_ * 4, 4)].reshape(4 * TOKS, 2 * HD), wo[...])
-        far = pl.multiple_of(af * TOKS, TOKS)
-        s1[k, 0] = part[k, pl.ds(far, 16), :].astype(BF)
-        go(remote(s1.at[k, 0], r1.at[k, 0], t1s.at[k, 0], t1r.at[k, 0], up_a))
-        s1[k, 1] = part[k, pl.ds(far + 16, 16), :].astype(BF)
-        go(remote(s1.at[k, 1], r1.at[k, 1], t1s.at[k, 1], t1r.at[k, 1], down_a))
+
+    def share(a_):
+        rows = jnp.concatenate([ain[b_ * 4 + a_] for b_ in order], axis=0)
+        return dot(rows, wo[...])
+
+    s1[...] = share(af).astype(BF).reshape(4, TOKS, D)
+    top_half, low_half = pl.ds(0, 16), pl.ds(16, 16)
     for k in range(4):
-        to_up = pl.multiple_of(ap * TOKS, TOKS)
-        await_bytes(r1.at[k, 0], t1r.at[k, 0])
-        s2[k, 0, 0:16] = (part[k, pl.ds(to_up, 16), :] + r1[k, 0].astype(F32)).astype(BF)
-        s2[k, 0, 16:32] = part[k, pl.ds(to_up + 16, 16), :].astype(BF)
-        go(remote(s2.at[k, 0], r2.at[k, 0], t2s.at[k, 0], t2r.at[k, 0], up_a))
-        to_down = pl.multiple_of(am * TOKS, TOKS)
-        await_bytes(r1.at[k, 1], t1r.at[k, 1])
-        s2[k, 1, 0:16] = part[k, pl.ds(to_down, 16), :].astype(BF)
-        s2[k, 1, 16:32] = (part[k, pl.ds(to_down + 16, 16), :] + r1[k, 1].astype(F32)).astype(BF)
-        go(remote(s2.at[k, 1], r2.at[k, 1], t2s.at[k, 1], t2r.at[k, 1], down_a))
-    mine = pl.multiple_of(a * TOKS, TOKS)
+        go(("s", k, 0), s1.at[k, top_half], r1.at[k, top_half], up_a)
+        go(("s", k, 1), s1.at[k, low_half], r1.at[k, low_half], down_a)
+    pup[...] = share(ap).reshape(4, TOKS, D)
+    pdown[...] = share(am).reshape(4, TOKS, D)
+    pown[...] = share(a).reshape(4, TOKS, D)
     for k in range(4):
-        await_bytes(r2.at[k, 0], t2r.at[k, 0])
-        await_bytes(r2.at[k, 1], t2r.at[k, 1])
-        rs = part[k, pl.ds(mine, TOKS), :] + r2[k, 0].astype(F32) + r2[k, 1].astype(F32)
-        if k == 0:
-            u1[0] = rs[0:16].astype(BF)
-            u1[1] = rs[16:32].astype(BF)
-            go(remote(u1.at[0], v1.at[0], p1s.at[0], p1r.at[0], up_b))
-            go(remote(u1.at[1], v1.at[1], p1s.at[1], p1r.at[1], down_b))
-        elif k == 1:
-            await_bytes(v1.at[0], p1r.at[0])
-            u2[0, 0:16] = (rs[0:16] + v1[0].astype(F32)).astype(BF)
-            u2[0, 16:32] = rs[16:32].astype(BF)
-            go(remote(u2.at[0], v2.at[0], p2s.at[0], p2r.at[0], up_b))
-        elif k == 2:
-            await_bytes(v1.at[1], p1r.at[1])
-            u2[1, 0:16] = rs[0:16].astype(BF)
-            u2[1, 16:32] = (rs[16:32] + v1[1].astype(F32)).astype(BF)
-            go(remote(u2.at[1], v2.at[1], p2s.at[1], p2r.at[1], down_b))
+        come(("s", k, 0), r1.at[k, top_half])
+        s2[k, 0, 0:16] = (pup[k, 0:16] + r1[k, 0:16].astype(F32)).astype(BF)
+        s2[k, 0, 16:32] = pup[k, 16:32].astype(BF)
+        go(("t", k, 0), s2.at[k, 0], r2.at[k, 0], up_a)
+        come(("s", k, 1), r1.at[k, low_half])
+        s2[k, 1, 0:16] = pdown[k, 0:16].astype(BF)
+        s2[k, 1, 16:32] = (pdown[k, 16:32] + r1[k, 16:32].astype(F32)).astype(BF)
+        go(("t", k, 1), s2.at[k, 1], r2.at[k, 1], down_a)
+    for k, b_ in enumerate(order):
+        come(("t", k, 0), r2.at[k, 0])
+        come(("t", k, 1), r2.at[k, 1])
+        rs = pown[k] + r2[k, 0].astype(F32) + r2[k, 1].astype(F32)
+        if k < 3:
+            v1[k] = rs.astype(BF)
+            go(("v", k), v1.at[k], v2.at[k], dev(a, b_))
         else:
-            rsum[...] = rs
-    await_bytes(v2.at[0], p2r.at[0])
-    await_bytes(v2.at[1], p2r.at[1])
-    hidden = res[...].astype(F32) + (
-        rsum[...] + v2[0].astype(F32) + v2[1].astype(F32)
-    )
-    rsum[...] = hidden
+            hid[...] = res[...].astype(F32) + rs
+    for k in range(3):
+        come(("v", k), v2.at[k])
+    hidden = hid[...] + (v2[0].astype(F32) + v2[1].astype(F32) + v2[2].astype(F32))
+    hid[...] = hidden
     inv = lax.rsqrt(jnp.mean(hidden * hidden, axis=-1, keepdims=True) + EPSILON)
     normed = (hidden * inv * ffn_gain[...][None, :]).astype(BF)
 
@@ -381,10 +385,10 @@
     fs[...] = drecv[...].reshape(1024, HD).astype(F32)
     for j in range(16):
         xs[:, HD * j : HD * (j + 1)] = fs[pl.ds(j, 64, stride=16), :].astype(BF)
-    gate = dot(xs[...], wg[...], NT)
-    up = dot(xs[...], wu[...], NT)
+    gate = dot(wg[...], xs[...], NT)
+    up = dot(wu[...], xs[...], NT)
     inner = (gate / (1.0 + jnp.exp(-gate)) * up).astype(BF)
-    y = dot(inner, wd[...])
+    y = dot(inner, wd[...], TN)
     for j in range(16):
         fs[pl.ds(j, 64, stride=16), :] = y[:, HD * j : HD * (j + 1)]
     ysend[...] = fs[...].astype(BF).reshape(N, 32, HD)
@@ -399,7 +403,7 @@
         yj = fs[pl.ds(j, 64, stride=16), :].astype(BF)
         moe = dot(comb_hi, yj, TN) + dot(comb_lo, yj, TN)
         cols = slice(HD * j, HD * (j + 1))
-        out_ref[:, cols] = (rsum[:, cols] + moe).astype(BF)
+        out_ref[:, cols] = (hid[:, cols] + moe).astype(BF)
 
     for copy in sends:
         copy.wait_send()
@@ -448,15 +452,15 @@
             vm((16, TOKS, 3 * HD), BF),
             vm((16, TOKS, 2 * HD), BF),
             vm((16, TOKS, 2 * HD), BF),
-            vm((4, 4 * TOKS, D), F32),
-            vm((4, 2, 16, D), BF),
-            vm((4, 2, 16, D), BF),
+            vm((4, TOKS, D), F32),
+            vm((4, TOKS, D), F32),
+            vm((4, TOKS, D), F32),
+            vm((4, TOKS, D), BF),
+            vm((4, TOKS, D), BF),
             vm((4, 2, TOKS, D), BF),
             vm((4, 2, TOKS, D), BF),
-            vm((2, 16, D), BF),
-            vm((2, 16, D), BF),
-            vm((2, TOKS, D), BF),
-            vm((2, TOKS, D), BF),
+            vm((3, TOKS, D), BF),
+            vm((3, TOKS, D), BF),
             vm((TOKS, D), F32),
             vm((1024, HD), F32),
             vm((2 * N, D), BF),
@@ -466,21 +470,16 @@
             vm((N, 32, HD), BF),
             vm((2 * N, TOKS), BF),
             vm((2 * N, TOKS), F32),
-            vm((TOKS, HD), F32),
-            vm((TOKS, HD), F32),
+            vm((TOKS, TOKS), BF),
+            vm((TOKS, HD), F32), vm((TOKS, HD), F32), vm((TOKS, HD), F32), vm((TOKS, HD), F32),
             vm((TOKS, TOKS), F32),
+            vm((1, CACHE), F32),
             dma((11,)),
             dma((10,)),
             pltpu.SemaphoreType.REGULAR,
-            dma((3,)), dma((3,)),
-            dma((10,)),
-            dma((2,)), dma((2,)),
-            dma((4, 2)), dma((4, 2)),
-            dma((10,)),
+            dma((40,)), dma((40,)),
             dma(()), dma(()),
             dma(()), dma((4,)),
-            dma((4, 2)), dma((4, 2)), dma((4, 2)), dma((4, 2)),
-            dma((2,)), dma((2,)), dma((2,)), dma((2,)),
             dma(()), dma(()), dma(()), dma(()),
         ],
         compiler_params=pltpu.CompilerParams(

time: 75.5 us -> 75.1 us (level)
  no operation moved by 1% of the time
where the time goes in v4:
time: 75.1 us; the launch traced here: 75 us
  Pallas kernels  71.4 us (95%)
  between operations  1.95 us (3%)
  local copies, waits for them, and re-layouts  1.57 us (2%)
    pallas_call x1, Pallas kernels, body(): pl.pallas_call(layer_kernel, out_shape=jax.ShapeDtypeStruct((TOKS, D), BF...  71.4 us
    unnamed x1, local copies, waits for them, and re-layouts  1.57 us

profile of v4, /device:TPU:1, one launch (start us, length us, event | category | flops | bytes accessed | tf_op | source)
XLA Modules:
  0.0 75.0 jit_solution(3178501359838698803)
XLA Ops:
  1.9 71.4 %layer.1 = bf16[32,2048]{1,0:T(8,128)(2,1)} custom-call(f32[1,128]{1,0:T(1,128)} %constant.2.clone.freq_hbm, f32[2048]{0:T(1024)} %again_hbm.1, f32[128]{0:T(128)} %qgain_hbm.1, f32[128]{0:T(128)} %kgain_hbm.1, f32[2048]{0:T(1024)} %fgain_hbm.1, s32[1,32]{1,0:T(1,128)} %par_hbm.1, s32[1]{0:T(128)S(6)} %copy.23.prefix_hbm, s32[1]{0:T(128)S(6)} %copy.24.acc_hbm, ...), custom_call_target="tpu_custom_call" | custom-call | tf_op jit(solution)/shard_map/layer/pallas_call | solution.py:429
  73.4 1.6 %copy.26 = bf16[32,2048]{1,0:T(8,128)(2,1)} copy(bf16[32,2048]{1,0:T(8,128)(2,1)} %layer.1) | data formatting | bytes 262144

commit v5 on v4

--- a/solution.py
+++ b/solution.py
@@ -47,7 +47,7 @@
     res, wq, wkv, wo, wg, wu, wd, kc, vc, ids, gates,
     ag, qsend, qrecv, asend, ain,
     pup, pdown, pown, s1, r1, s2, r2, v1, v2, hid,
-    fs, xs, dsend, drecv, ysend, yrecv, sel_ref, comb_ref, link_ref,
+    fs, xs, dsend, drecv, ysend, yrecv, sel_ref, comb_ref,
     qcos, qsin, kcos, ksin, allow_ref, seen_ref,
     lsem, isem, meet, snd, rcv, qs, qr, asem, ar, ds, dr, ys, yr,
 ):
@@ -136,32 +136,6 @@
     inv = lax.rsqrt(jnp.mean(xv * xv, axis=-1, keepdims=True) + EPSILON)
     ag[own] = (xv * inv * attn_gain[...][None, :]).astype(BF)
 
-    for load in loads[2:4] + small[1:]:
-        load.wait()
-    line = lax.broadcasted_iota(jnp.int32, (2 * N, TOKS), 0)
-    expert = line // 2
-    named = jnp.zeros((2 * N, TOKS), F32)
-    weight = jnp.zeros((2 * N, TOKS), F32)
-    turn_lanes = lax.rem(HD - lax.rem(t, 4) * TOKS, HD)
-    idv = pltpu.roll(ids[...], turn_lanes, 1)[:, 0:TOKS]
-    gv = pltpu.roll(gates[...], turn_lanes, 1)[:, 0:TOKS]
-    for k in range(8):
-        hit = jnp.broadcast_to(idv[k : k + 1], (2 * N, TOKS)) == expert
-        named = jnp.where(hit, 1.0, named)
-        weight = weight + jnp.where(hit, jnp.broadcast_to(gv[k : k + 1], (2 * N, TOKS)), 0.0)
-    ri = lax.broadcasted_iota(jnp.int32, (TOKS, TOKS), 0)
-    ci = lax.broadcasted_iota(jnp.int32, (TOKS, TOKS), 1)
-    before = dot(named.astype(BF), jnp.where(ri < ci, 1.0, 0.0).astype(BF))
-    turn = lax.rem(line, 2).astype(F32)
-    taken = (named > 0.5) & (jnp.abs(before - turn) < 0.5)
-    sel_ref[...] = jnp.where(taken, 1.0, 0.0).astype(BF)
-    comb_ref[...] = jnp.where(taken, weight, 0.0)
-
-    link = jnp.where((ri == jnp.broadcast_to(parents[...], (TOKS, TOKS))) | (ri == ci), 1.0, 0.0)
-    for unused in range(5):
-        link = jnp.minimum(dot(link.astype(BF), link.astype(BF)), 1.0)
-    link_ref[...] = link.astype(BF)
-
     pl.semaphore_wait(barrier, 7)
 
     up_a, down_a = dev(ring(a, 1), b), dev(ring(a, 3), b)
@@ -187,8 +161,15 @@
     go("wkv", wkv_hbm, wkv.at[pl.ds(kv_row, 32)], sibling)
     go("wo", wo_hbm, wo.at[pl.ds(lane0, HD)], sibling)
 
+    for load in small[1:]:
+        load.wait()
+    ri = lax.broadcasted_iota(jnp.int32, (TOKS, TOKS), 0)
+    ci = lax.broadcasted_iota(jnp.int32, (TOKS, TOKS), 1)
+    link = jnp.where((ri == jnp.broadcast_to(parents[...], (TOKS, TOKS))) | (ri == ci), 1.0, 0.0)
+    for unused in range(5):
+        link = jnp.minimum(dot(link.astype(BF), link.astype(BF)), 1.0)
     eye = jnp.where(ri == ci, 1.0, 0.0).astype(BF)
-    reach = dot(link_ref[...], eye, TN)
+    reach = dot(link.astype(BF), eye, TN)
     allowed = jnp.where(kind[0] == 1, reach, jnp.where(ci <= ri, 1.0, 0.0))
     allow_ref[...] = jnp.where(allowed > 0.5, 0.0, NEG_FILL)
     depth = jnp.sum(allowed, axis=1, keepdims=True) - 1.0
@@ -285,7 +266,8 @@
         )
         return (turned.reshape(count * TOKS, HD) * lax.rsqrt(mean + EPSILON)).astype(BF)
 
-    def heads(g, carry):
+    def heads(off):
+        g = ring(cx, off)
         qraw = [
             qrecv[4 * g + i, :, HD * j : HD * (j + 1)] for i in range(4) for j in range(2)
         ]
@@ -311,13 +293,16 @@
                 r0 = (2 * i + j) * TOKS
                 asend[to, :, HD * j : HD * (j + 1)] = o[r0 : r0 + TOKS]
 
-            @pl.when(to != chip)
-            def _():
+            def send():
                 remote(asend.at[to], ain.at[own], asem, ar.at[b], 2 * to + core).start()
 
-        return carry
-
-    lax.fori_loop(0, 4, heads, 0)
+            if off == 0:
+                pl.when(to != chip)(send)
+            else:
+                send()
+
+    for off in (2, 1, 3, 0):
+        heads(off)
     ain[own] = asend[chip]
 
     loads[4].wait()
@@ -338,6 +323,26 @@
     pup[...] = share(ap).reshape(4, TOKS, D)
     pdown[...] = share(am).reshape(4, TOKS, D)
     pown[...] = share(a).reshape(4, TOKS, D)
+
+    for load in loads[2:4]:
+        load.wait()
+    line = lax.broadcasted_iota(jnp.int32, (2 * N, TOKS), 0)
+    expert = line // 2
+    named = jnp.zeros((2 * N, TOKS), F32)
+    weight = jnp.zeros((2 * N, TOKS), F32)
+    turn_lanes = lax.rem(HD - lax.rem(t, 4) * TOKS, HD)
+    idv = pltpu.roll(ids[...], turn_lanes, 1)[:, 0:TOKS]
+    gv = pltpu.roll(gates[...], turn_lanes, 1)[:, 0:TOKS]
+    for k in range(8):
+        hit = jnp.broadcast_to(idv[k : k + 1], (2 * N, TOKS)) == expert
+        named = jnp.where(hit, 1.0, named)
+        weight = weight + jnp.where(hit, jnp.broadcast_to(gv[k : k + 1], (2 * N, TOKS)), 0.0)
+    before = dot(named.astype(BF), jnp.where(ri < ci, 1.0, 0.0).astype(BF))
+    turn = lax.rem(line, 2).astype(F32)
+    taken = (named > 0.5) & (jnp.abs(before - turn) < 0.5)
+    sel_ref[...] = jnp.where(taken, 1.0, 0.0).astype(BF)
+    comb_ref[...] = jnp.where(taken, weight, 0.0)
+
     for k in range(4):
         come(("s", k, 0), r1.at[k, top_half])
         s2[k, 0, 0:16] = (pup[k, 0:16] + r1[k, 0:16].astype(F32)).astype(BF)
@@ -470,7 +475,6 @@
             vm((N, 32, HD), BF),
             vm((2 * N, TOKS), BF),
             vm((2 * N, TOKS), F32),
-            vm((TOKS, TOKS), BF),
             vm((TOKS, HD), F32), vm((TOKS, HD), F32), vm((TOKS, HD), F32), vm((TOKS, HD), F32),
             vm((TOKS, TOKS), F32),
             vm((1, CACHE), F32),

time: 75.1 us -> 73.5 us (0.979)
  Pallas kernels: 71.4 us -> 69.9 us
    pallas_call x1, Pallas kernels: 71.4 us -> 69.9 us  [body(): pl.pallas_call(layer_kernel, out_shape=jax.ShapeDtypeStruct((TOKS, D), BF...]
where the time goes in v5:
time: 73.5 us; the launch traced here: 73.4 us
  Pallas kernels  69.9 us (95%)
  between operations  1.95 us (3%)
  local copies, waits for them, and re-layouts  1.57 us (2%)
    pallas_call x1, Pallas kernels, body(): pl.pallas_call(layer_kernel, out_shape=jax.ShapeDtypeStruct((TOKS, D), BF...  69.9 us
    unnamed x1, local copies, waits for them, and re-layouts  1.57 us

profile of v5, /device:TPU:1, one launch (start us, length us, event | category | flops | bytes accessed | tf_op | source)
XLA Modules:
  0.0 73.4 jit_solution(7351281356476714685)
XLA Ops:
  1.9 69.9 %layer.1 = bf16[32,2048]{1,0:T(8,128)(2,1)} custom-call(f32[1,128]{1,0:T(1,128)} %constant.2.clone.freq_hbm, f32[2048]{0:T(1024)} %again_hbm.1, f32[128]{0:T(128)} %qgain_hbm.1, f32[128]{0:T(128)} %kgain_hbm.1, f32[2048]{0:T(1024)} %fgain_hbm.1, s32[1,32]{1,0:T(1,128)} %par_hbm.1, s32[1]{0:T(128)S(6)} %copy.23.prefix_hbm, s32[1]{0:T(128)S(6)} %copy.24.acc_hbm, ...), custom_call_target="tpu_custom_call" | custom-call | tf_op jit(solution)/shard_map/layer/pallas_call | solution.py:434
  71.9 1.6 %copy.26 = bf16[32,2048]{1,0:T(8,128)(2,1)} copy(bf16[32,2048]{1,0:T(8,128)(2,1)} %layer.1) | data formatting | bytes 262144

commit v6 on v5

--- a/solution.py
+++ b/solution.py
@@ -44,7 +44,7 @@
     res_hbm, wq_hbm, wkv_hbm, wo_hbm, wg_hbm, wu_hbm, wd_hbm, kc_hbm, vc_hbm, ids_hbm, gates_hbm,
     out_ref,
     freq_ref, attn_gain, query_gain, key_gain, ffn_gain, parents, prefix, accepted, path, kind,
-    res, wq, wkv, wo, wg, wu, wd, kc, vc, ids, gates,
+    res, wq, wkv, wo, wg, wu, wd, wgt, wut, kc, vc, ids, gates,
     ag, qsend, qrecv, asend, ain,
     pup, pdown, pown, s1, r1, s2, r2, v1, v2, hid,
     fs, xs, dsend, drecv, ysend, yrecv, sel_ref, comb_ref,
@@ -212,40 +212,48 @@
     come("wq", wq.at[:, pl.ds(other_lane, HD)])
     come("wkv", wkv.at[pl.ds(other_row, 32)])
 
-    def project(b_):
-        rows = ag[pl.ds(b_ * 4, 4)].reshape(4 * TOKS, D)
-        q = dot(rows, wq[...])
-        kv = dot(rows, wkv[...], NT)
-        qsend[pl.ds(b_ * 4, 4), :, 0 : 2 * HD] = q.astype(BF).reshape(4, TOKS, 2 * HD)
-        qsend[pl.ds(b_ * 4, 4), :, 2 * HD :] = kv.astype(BF).reshape(4, TOKS, HD)
-
-    def post_queries(b_, first):
-        for k in (2, 1, 3, 0)[: 4 - first]:
-            a_ = ring(a, k)
-            copy = remote(
-                qsend.at[b_ * 4 + a_], qrecv.at[chip], qs, qr, dev(a_, b_)
-            )
-            copy.start()
-
-    project(b)
+    def project(blocks):
+        count = len(blocks)
+        rows = jnp.concatenate([ag[b_ * 4 + a_] for a_, b_ in blocks], axis=0)
+        q = dot(rows, wq[...]).astype(BF)
+        kv = dot(rows, wkv[...], NT).astype(BF)
+        for i in range(count):
+            a_, b_ = blocks[i]
+            r = slice(TOKS * i, TOKS * (i + 1))
+            qsend[b_ * 4 + a_, :, 0 : 2 * HD] = q[r]
+            qsend[b_ * 4 + a_, :, 2 * HD :] = kv[r]
+
+    def post_queries(blocks):
+        for a_, b_ in blocks:
+            remote(qsend.at[b_ * 4 + a_], qrecv.at[chip], qs, qr, dev(a_, b_)).start()
+
+    near = [(af, b), (ap, b), (am, b)]
+    project(near + [(a, b)])
     qrecv[chip] = qsend[own]
-    post_queries(b, 1)
+    post_queries(near)
 
     relay_b(1, am)
     relay_b(2, ap)
+    near = [(a_, b_) for a_ in (ap, am, a) for b_ in (bm, bp)]
+    project(near)
+    post_queries(near)
     come(("b", 3, 0), blk(af, bm))
-    project(bm)
-    post_queries(bm, 0)
     come(("b", 3, 1), blk(af, bp))
-    project(bp)
-    post_queries(bp, 0)
     for j, a_ in enumerate((a, am, ap)):
         come(("bh", j, 0), half(a_, bf, 0))
         come(("bh", j, 1), half(a_, bf, 1))
     come(("b", 3, 2), blk(af, bf))
+    rest = [(af, bf), (ap, bf), (am, bf), (af, bm), (af, bp), (a, bf)]
     pl.semaphore_signal(meet, inc=1, device_id={"tensor": sibling}, device_id_type=MESH)
-    project(bf)
-    post_queries(bf, 0)
+    project(rest)
+    post_queries(rest)
+
+    def turn_weights(src, dst):
+        for i in range(FF // HD):
+            dst[:, HD * i : HD * (i + 1)] = src[HD * i : HD * (i + 1), :].T
+
+    loads[7].wait()
+    turn_weights(wg, wgt)
 
     for load in loads[5:7]:
         load.wait()
@@ -304,6 +312,8 @@
     for off in (2, 1, 3, 0):
         heads(off)
     ain[own] = asend[chip]
+    loads[8].wait()
+    turn_weights(wu, wut)
 
     loads[4].wait()
     come("wo", wo.at[pl.ds(other_lane, HD)])
@@ -384,16 +394,15 @@
     pl.semaphore_wait(meet, 1)
     post(dsend, drecv, ds, dr)
     drecv[t] = dsend[t]
-    for load in loads[7:]:
-        load.wait()
+    loads[9].wait()
     await_bytes(drecv.at[pl.ds(0, N - 1)], dr)
     fs[...] = drecv[...].reshape(1024, HD).astype(F32)
     for j in range(16):
         xs[:, HD * j : HD * (j + 1)] = fs[pl.ds(j, 64, stride=16), :].astype(BF)
-    gate = dot(wg[...], xs[...], NT)
-    up = dot(wu[...], xs[...], NT)
+    gate = dot(xs[...], wgt[...])
+    up = dot(xs[...], wut[...])
     inner = (gate / (1.0 + jnp.exp(-gate)) * up).astype(BF)
-    y = dot(inner, wd[...], TN)
+    y = dot(inner, wd[...])
     for j in range(16):
         fs[pl.ds(j, 64, stride=16), :] = y[:, HD * j : HD * (j + 1)]
     ysend[...] = fs[...].astype(BF).reshape(N, 32, HD)
@@ -448,6 +457,8 @@
             vm((FF, D), BF),
             vm((FF, D), BF),
             vm((FF, D), BF),
+            vm((D, FF), BF),
+            vm((D, FF), BF),
             vm((CACHE, 4 * HD), BF),
             vm((CACHE, 4 * HD), BF),
             vm((8, HD), jnp.int32),

time: 73.5 us -> 72.9 us (level)
  no operation moved by 1% of the time
where the time goes in v6:
time: 72.9 us; the launch traced here: 72.8 us
  Pallas kernels  69.2 us (95%)
  between operations  1.95 us (3%)
  local copies, waits for them, and re-layouts  1.57 us (2%)
    pallas_call x1, Pallas kernels, body(): pl.pallas_call(layer_kernel, out_shape=jax.ShapeDtypeStruct((TOKS, D), BF...  69.2 us
    unnamed x1, local copies, waits for them, and re-layouts  1.57 us

profile of v6, /device:TPU:1, one launch (start us, length us, event | category | flops | bytes accessed | tf_op | source)
XLA Modules:
  0.0 72.8 jit_solution(17314303757731290209)
XLA Ops:
  1.9 69.2 %layer.1 = bf16[32,2048]{1,0:T(8,128)(2,1)} custom-call(f32[1,128]{1,0:T(1,128)} %constant.2.clone.freq_hbm, f32[2048]{0:T(1024)} %again_hbm.1, f32[128]{0:T(128)} %qgain_hbm.1, f32[128]{0:T(128)} %kgain_hbm.1, f32[2048]{0:T(1024)} %fgain_hbm.1, s32[1,32]{1,0:T(1,128)} %par_hbm.1, s32[1]{0:T(128)S(6)} %copy.23.prefix_hbm, s32[1]{0:T(128)S(6)} %copy.24.acc_hbm, ...), custom_call_target="tpu_custom_call" | custom-call | tf_op jit(solution)/shard_map/layer/pallas_call | solution.py:443
  71.2 1.6 %copy.26 = bf16[32,2048]{1,0:T(8,128)(2,1)} copy(bf16[32,2048]{1,0:T(8,128)(2,1)} %layer.1) | data formatting | bytes 262144

commit v7 on v6

--- a/solution.py
+++ b/solution.py
@@ -408,22 +408,21 @@
     ysend[...] = fs[...].astype(BF).reshape(N, 32, HD)
     post(ysend, yrecv, ys, yr)
     yrecv[t] = ysend[t]
-    await_bytes(yrecv.at[pl.ds(0, N - 1)], yr)
-    fs[...] = yrecv[...].reshape(1024, HD).astype(F32)
+    for copy in sends:
+        copy.wait_send()
+    await_bytes(qsend.at[pl.ds(0, 15)], qs)
+    await_bytes(asend.at[pl.ds(0, 15)], asem)
+    await_bytes(dsend.at[pl.ds(0, N - 1)], ds)
     comb = comb_ref[...]
     comb_hi = comb.astype(BF)
     comb_lo = (comb - comb_hi.astype(F32)).astype(BF)
+    await_bytes(yrecv.at[pl.ds(0, N - 1)], yr)
+    fs[...] = yrecv[...].reshape(1024, HD).astype(F32)
     for j in range(16):
         yj = fs[pl.ds(j, 64, stride=16), :].astype(BF)
         moe = dot(comb_hi, yj, TN) + dot(comb_lo, yj, TN)
         cols = slice(HD * j, HD * (j + 1))
         out_ref[:, cols] = (hid[:, cols] + moe).astype(BF)
-
-    for copy in sends:
-        copy.wait_send()
-    await_bytes(qsend.at[pl.ds(0, 15)], qs)
-    await_bytes(asend.at[pl.ds(0, 15)], asem)
-    await_bytes(dsend.at[pl.ds(0, N - 1)], ds)
     await_bytes(ysend.at[pl.ds(0, N - 1)], ys)
 
 
@@ -442,7 +441,7 @@
     vm = pltpu.VMEM
     return pl.pallas_call(
         layer_kernel,
-        out_shape=jax.ShapeDtypeStruct((TOKS, D), BF),
+        out_shape=pltpu.VMEM((TOKS, D), BF),
         in_specs=[hbm] * 21,
         out_specs=vmem,
         scratch_shapes=[

time: 72.9 us -> 71.2 us (0.977)
  local copies, waits for them, and re-layouts: 1.57 us -> 0.66 us
    unnamed x1, local copies, waits for them, and re-layouts: 1.57 us -> 0.66 us
where the time goes in v7:
time: 71.2 us; the launch traced here: 71.1 us
  Pallas kernels  68.5 us (96%)
  between operations  1.95 us (3%)
    pallas_call x1, Pallas kernels, body(): pl.pallas_call(layer_kernel, out_shape=pltpu.VMEM((TOKS, D), BF), in_spec...  68.5 us

profile of v7, /device:TPU:1, one launch (start us, length us, event | category | flops | bytes accessed | tf_op | source)
XLA Modules:
  0.0 71.1 jit_solution(16595708544260994741)
XLA Ops:
  1.9 68.5 %layer.1 = bf16[32,2048]{1,0:T(8,128)(2,1)S(1)} custom-call(f32[1,128]{1,0:T(1,128)} %constant.2.clone.freq_hbm, f32[2048]{0:T(1024)} %again_hbm.1, f32[128]{0:T(128)} %qgain_hbm.1, f32[128]{0:T(128)} %kgain_hbm.1, f32[2048]{0:T(1024)} %fgain_hbm.1, s32[1,32]{1,0:T(1,128)} %par_hbm.1, s32[1]{0:T(128)S(6)} %copy.24.prefix_hbm, s32[1]{0:T(128)S(6)} %copy.25.acc_hbm, ...), custom_call_target="tpu_custom_call" | custom-call | tf_op jit(solution)/shard_map/layer/pallas_call | solution.py:442
  70.5 0.7 copy.23

commit v8 on v7

--- a/solution.py
+++ b/solution.py
@@ -155,8 +155,8 @@
     bm, bp, bf = ring(b, 3), ring(b, 1), ring(b, 2)
     go(("a", 0), blk(a, b), blk(a, b), up_a)
     go(("a", 1), blk(a, b), blk(a, b), down_a)
+    go(("a", 2), blk(a, b), blk(a, b), dev(af, b))
     spread_b(0, a)
-    go(("a", 2), blk(a, b), blk(a, b), dev(af, b))
     go("wq", wq_hbm, wq.at[:, pl.ds(lane0, HD)], sibling)
     go("wkv", wkv_hbm, wkv.at[pl.ds(kv_row, 32)], sibling)
     go("wo", wo_hbm, wo.at[pl.ds(lane0, HD)], sibling)

time: 71.2 us -> 71.2 us (level)
  no operation moved by 1% of the time
where the time goes in v8:
time: 71.2 us; the launch traced here: 71.1 us
  Pallas kernels  68.5 us (96%)
  between operations  1.95 us (3%)
    pallas_call x1, Pallas kernels, body(): pl.pallas_call(layer_kernel, out_shape=pltpu.VMEM((TOKS, D), BF), in_spec...  68.5 us

profile of v8, /device:TPU:1, one launch (start us, length us, event | category | flops | bytes accessed | tf_op | source)
XLA Modules:
  0.0 71.1 jit_solution(9503834467191242277)
XLA Ops:
  1.9 68.5 %layer.1 = bf16[32,2048]{1,0:T(8,128)(2,1)S(1)} custom-call(f32[1,128]{1,0:T(1,128)} %constant.2.clone.freq_hbm, f32[2048]{0:T(1024)} %again_hbm.1, f32[128]{0:T(128)} %qgain_hbm.1, f32[128]{0:T(128)} %kgain_hbm.1, f32[2048]{0:T(1024)} %fgain_hbm.1, s32[1,32]{1,0:T(1,128)} %par_hbm.1, s32[1]{0:T(128)S(6)} %copy.24.prefix_hbm, s32[1]{0:T(128)S(6)} %copy.25.acc_hbm, ...), custom_call_target="tpu_custom_call" | custom-call | tf_op jit(solution)/shard_map/layer/pallas_call | solution.py:442
  70.5 0.7 copy.23
